TPU v7x, 512 devices: a whole 4x8x8 slice. The times are simulated.
512 devices in a mesh: mesh: 32 (over x_hi, z, core), band: 16 (over x_lo, y).
Axes of the slice: x: 4 (x_hi: 2, x_lo: 2; x = x_hi * 2 + x_lo), y: 8, z: 8, core: 2. Of those that a mesh axis runs over, the one named last changes fastest.
Arguments:
- filter_block: bfloat16 [512, 196608], P('band', 'mesh'), may hold values from -6 to 6
- local_pot: float32 [196608], P('mesh'), may hold values from 0.5 to 2
- cell_scale: float32 [4096], P('mesh'), may hold values from 0.5 to 2
- cell_kernel: bfloat16 [125, 125], replicated
- cell_map: int32 [125, 4096], P(None, 'mesh'), may hold values from 0 to 8191, as said below
- neighbour_ids: int32 [32, 14], P('mesh'), may hold values from 0 to 31, as said below
- send_nodes: int32 [32, 14, 64], P('mesh'), may hold values from 0 to 6143
- rotation_rows: bfloat16 [512, 512], P('band'), may hold values from -0.25 to 0.25
- panel_owner: int32 [2], replicated, may hold values from 0 to 15
Outputs:
- filtered: bfloat16 [512, 196608], P('band', 'mesh')
- rotated: bfloat16 [512, 196608], P(None, ('mesh', 'band'))
- state_energy: float32 [512], P('band')
Inputs may be any that keep to these rules, and one draw needn't show every extreme that they name: `neighbour_ids`: row p lists 14 distinct partitions other than p; q is listed in row p exactly when p is listed in row q. `cell_map`: in the columns of partition p's cells an entry below 6144 names an owned node of p, and an entry 6144 + q*64 + g names slot g of a partition q listed in row p of neighbour_ids.
All inputs are finite; a program needn't handle non-finite values.
Results may differ from a plain program's by a relative error of at most 0.0059.
Values may be sent and summed in bfloat16 or wider, within the bound.
No kernel may reach another device: no remote copies, remote signals or barrier semaphores. Data moves between devices by JAX's collectives and lax.ppermute only.
A program may use at most 64 MiB of HBM per device.

v0:
```python
import jax
import jax.numpy as jnp
from jax import lax
from jax.sharding import PartitionSpec as P

center = 6.0
half_width = 4.0


def spread(value, axis, root):
    mine = lax.axis_index(axis) == root
    return lax.psum(jnp.where(mine, value, jnp.zeros_like(value)), axis)


def import_ghosts(state_field, neighbour_ids, send_nodes):
    count = state_field.shape[0]
    mesh_size = lax.axis_size("mesh")
    lists = send_nodes[0]
    packed = jnp.take(state_field, lists.reshape(-1), axis=1).reshape(
        count, lists.shape[0], lists.shape[1]
    )
    placement = (
        neighbour_ids[0][None, :] == jnp.arange(mesh_size, dtype=jnp.int32)[:, None]
    ).astype(jnp.bfloat16)
    outgoing = jnp.einsum("qr,srg->sqg", placement, packed, preferred_element_type=jnp.float32)
    outgoing = outgoing.astype(jnp.bfloat16).reshape(count, mesh_size * lists.shape[1])
    return lax.all_to_all(outgoing, "mesh", split_axis=1, concat_axis=1, tiled=True)


def apply_cells(state_field, ghosts, cell_map, cell_scale, cell_kernel, local_pot):
    count = state_field.shape[0]
    extended = jnp.concatenate([state_field, ghosts], axis=1)
    cells = cell_map.shape[1]
    width = 128

    def add_block(block_id, totals):
        gathered = jnp.take(extended, cell_map, axis=1)
        product = (
            jnp.einsum("ab,sbc->sac", cell_kernel, gathered, preferred_element_type=jnp.float32)
            * cell_scale
        )
        return totals.at[:, cell_map.reshape(-1)].add(product.reshape(count, -1))

    totals = lax.fori_loop(
        0, cells // width, add_block, jnp.zeros((count, extended.shape[1]), jnp.float32)
    )
    return totals[:, : state_field.shape[1]] + local_pot * state_field.astype(jnp.float32)


def per_device(
    filter_block,
    local_pot,
    cell_scale,
    cell_kernel,
    cell_map,
    neighbour_ids,
    send_nodes,
    rotation_rows,
    panel_owner,
):
    count = filter_block.shape[0]
    node_count = filter_block.shape[1]
    ghosts_zero = import_ghosts(filter_block, neighbour_ids, send_nodes)
    image_zero = apply_cells(
        filter_block, ghosts_zero, cell_map, cell_scale, cell_kernel, local_pot
    )
    start_field = filter_block.astype(jnp.float32)
    field_one = ((image_zero - center * start_field) / half_width).astype(jnp.bfloat16)
    ghosts_one = import_ghosts(field_one, neighbour_ids, send_nodes)
    image_one = apply_cells(field_one, ghosts_one, cell_map, cell_scale, cell_kernel, local_pot)
    one_float = field_one.astype(jnp.float32)
    energy_local = jnp.sum(one_float * image_one, axis=1)
    state_energy = lax.psum(energy_local, "mesh") / (node_count * lax.axis_size("mesh"))
    filtered = (2.0 * (image_one - center * one_float) / half_width - start_field).astype(
        jnp.bfloat16
    )
    band_index = lax.axis_index("band")
    totals = jnp.zeros((count, node_count), jnp.float32)
    for step_id in range(panel_owner.shape[0]):
        owner_id = panel_owner[step_id]
        panel_rows, coefficients = (
            spread(filtered, "band", owner_id),
            spread(rotation_rows, "band", owner_id),
        )
        my_coeff = lax.dynamic_slice_in_dim(coefficients, band_index * count, count, 1)
        totals = totals + lax.dot_general(
            my_coeff, panel_rows, (((0,), (0,)), ((), ())), preferred_element_type=jnp.float32
        )
    rotated = lax.all_to_all(
        totals.astype(jnp.bfloat16), "band", split_axis=1, concat_axis=0, tiled=True
    )
    return (filtered, rotated, state_energy)


def solution(mesh):
    placed = (
        P("band", "mesh"),
        P("mesh"),
        P("mesh"),
        P(),
        P(None, "mesh"),
        P("mesh", None),
        P("mesh", None, None),
        P("band", None),
        P(),
    )
    return jax.shard_map(
        per_device,
        mesh=mesh,
        in_specs=placed,
        out_specs=(P("band", "mesh"), P(None, ("mesh", "band")), P("band")),
        check_vma=False,
    )
```

profile of v0, /device:TPU:1, one launch (start us, length us, event | category | flops | bytes accessed | tf_op | source)
XLA Modules:
  0.0 586.1 jit_solution(6546649709300623704)
XLA Ops:
  8.1 1.8 copy.84
  9.9 2.4 gather_fusion
  13.9 14.4 %all-to-all-start = ((bf16[32,2,1024]{2,1,0:T(2,128)(2,1)}), bf16[32,2,1024]{2,1,0:T(2,128)(2,1)S(1)}, u32[]{:S(2)}, u32[]{:S(2)}) async-start(bf16[32,2,1024]{2,1,0:T(2,128)(2,1)} %reshape.156), calls=%async_computation | async-start | bytes 262144 | tf_op jit(solution)/shard_map/all_to_all | solution.py:27
  28.8 10.2 %all-to-all-done = bf16[32,2,1024]{2,1,0:T(2,128)(2,1)S(1)} async-done(((bf16[32,2,1024]{2,1,0:T(2,128)(2,1)}), bf16[32,2,1024]{2,1,0:T(2,128)(2,1)S(1)}, u32[]{:S(2)}, u32[]{:S(2)}) %all-to-all-start) | async-done | bytes 131104 | tf_op jit(solution)/shard_map/all_to_all | solution.py:27
  40.7 32.9 %gather_fusion.1 = bf16[16000,32]{1,0:T(8,128)(2,1)} fusion(bf16[32,8192]{0,1:T(8,128)(2,1)S(1)} %copy.88, s32[16384]{0:T(1024)S(1)} %pad_clamp_fusion), kind=kCustom, calls=%fused_computation.1.clone | custom fusion | bytes 2112000 | tf_op jit(solution)/shard_map/while/body/eval_jaxpr/jit(_take)/gather | solution.py:37
  73.6 6.2 %copy.89 = bf16[125,128,32]{0,1,2:T(8,128)(2,1)S(1)} copy(bf16[125,128,32]{2,1,0:T(8,128)(2,1)} %bitcast.81) | data formatting | bytes 2048000 | tf_op jit(solution)/shard_map/while/body/eval_jaxpr/jit(_take)/gather | solution.py:37
  80.3 1.9 copy.90
  82.2 2.8 copy.115
  85.0 4.7 copy.91
  89.7 90.3 %scatter_custom_fusion = f32[32,8192]{0,1:T(8,128)} fusion(s32[16000]{0:T(1024)S(1)} %fusion.24, f32[16000,32]{1,0:T(8,128)} %copy.91, f32[]{:T(128)} %constant.27.clone.1), kind=kCustom, calls=%fused_computation.28 | custom fusion | flops 512000 | bytes 1049088 | tf_op jit(solution)/shard_map/while/body/eval_jaxpr/scatter-add | solution.py:42
  180.0 2.4 fusion.4
  182.4 2.4 gather_fusion.2
  186.5 5.3 all-to-all-start.1
  194.5 8.0 %all-to-all-done.1 = bf16[32,2,1024]{2,1,0:T(2,128)(2,1)S(1)} async-done(((bf16[32,2,1024]{2,1,0:T(2,128)(2,1)}), bf16[32,2,1024]{2,1,0:T(2,128)(2,1)S(1)}, u32[]{:S(2)}, u32[]{:S(2)}) %all-to-all-start.1) | async-done | bytes 131104 | tf_op jit(solution)/shard_map/all_to_all | solution.py:27
  203.0 1.8 pad_maximum_fusion
  204.8 32.9 %gather_fusion.3 = bf16[16000,32]{1,0:T(8,128)(2,1)} fusion(bf16[32,8192]{0,1:T(8,128)(2,1)S(1)} %pad_maximum_fusion, s32[16384]{0:T(1024)S(1)} %pad_clamp_fusion), kind=kCustom, calls=%fused_computation.3.clone | custom fusion | bytes 2112000 | tf_op jit(solution)/shard_map/while/body/eval_jaxpr/jit(_take)/gather | solution.py:37
  237.8 6.2 %copy.97 = bf16[125,128,32]{0,1,2:T(8,128)(2,1)S(1)} copy(bf16[125,128,32]{2,1,0:T(8,128)(2,1)} %bitcast.80) | data formatting | bytes 2048000 | tf_op jit(solution)/shard_map/while/body/eval_jaxpr/jit(_take)/gather | solution.py:37
  244.4 1.9 copy.98
  246.4 2.8 copy.114
  249.2 4.7 copy.99
  253.9 90.3 %scatter_custom_fusion.1 = f32[32,8192]{0,1:T(8,128)} fusion(s32[16000]{0:T(1024)S(1)} %fusion.24, f32[16000,32]{1,0:T(8,128)} %copy.99, f32[]{:T(128)} %constant.27.clone.1), kind=kCustom, calls=%fused_computation.26 | custom fusion | flops 512000 | bytes 1049088 | tf_op jit(solution)/shard_map/while/body/eval_jaxpr/scatter-add | solution.py:42
  344.2 3.6 broadcast_select_fusion
  347.7 1.1 copy-done.6
  348.9 1.3 broadcast_select_fusion.1
  350.2 138.9 %all-reduce.7.cloned.1.call-done = (bf16[32,6144]{0,1:T(8,128)(2,1)}, bf16[32,6144]{0,1:T(8,128)(2,1)}) async-done(((bf16[32,6144]{0,1:T(8,128)(2,1)}, bf16[32,6144]{0,1:T(8,128)(2,1)}), (bf16[32,6144]{0,1:T(8,128)(2,1)}, bf16[32,6144]{0,1:T(8,128)(2,1)})) %all-reduce.7.cloned.1.call-update) | async-done | bytes 786448 | tf_op jit(solution)/shard_map/psum | solution.py:12
  489.1 2.3 fusion.29
  491.4 1.4 fusion
  493.6 4.2 all-to-all-start.2
  497.8 1.3 copy.101
  499.1 2.4 fusion.9
  501.5 75.4 %psum.39 = f32[32]{0:T(128)S(1)} all-reduce(f32[32]{0:T(128)S(1)} %fusion.9), channel_id=1, replica_groups=mesh['mesh'=32,'band'=16] {'mesh'}, use_global_device_ids=true, to_apply=%region_7.10 | all-reduce | flops 32 | bytes 256 | tf_op jit(solution)/shard_map/psum | solution.py:73
  577.5 1.8 copy.124
  (70 shorter events, 10.3 us)
Async XLA Ops:
  7.2 72.7 %copy-start = (bf16[125,125]{1,0:T(8,128)(2,1)S(1)}, bf16[125,125]{1,0:T(8,128)(2,1)}, u32[]{:S(2)}) copy-start(bf16[125,125]{1,0:T(8,128)(2,1)} %param.16) | copy-start | bytes 93754
  7.2 5.4 copy-start.13
  7.2 21.2 %copy-start.10 = (s32[125,128]{1,0:T(8,128)S(1)}, s32[125,128]{1,0:T(8,128)}, u32[]{:S(2)}) copy-start(s32[125,128]{1,0:T(8,128)} %param.17) | copy-start | bytes 192004
  8.0 31.5 %copy-start.9 = (bf16[32,6144]{1,0:T(8,128)(2,1)S(1)}, bf16[32,6144]{1,0:T(8,128)(2,1)}, u32[]{:S(2)}) copy-start(bf16[32,6144]{1,0:T(8,128)(2,1)} %param.13) | copy-start | bytes 1179652
  9.8 29.7 %copy-start.3 = (bf16[32,6144]{0,1:T(8,128)(2,1)}, bf16[32,6144]{0,1:T(8,128)(2,1)S(1)}, u32[]{:S(2)}) copy-start(bf16[32,6144]{0,1:T(8,128)(2,1)S(1)} %copy.84) | copy-start | bytes 1179652
  13.9 25.0 %all-to-all-start = ((bf16[32,2,1024]{2,1,0:T(2,128)(2,1)}), bf16[32,2,1024]{2,1,0:T(2,128)(2,1)S(1)}, u32[]{:S(2)}, u32[]{:S(2)}) async-start(bf16[32,2,1024]{2,1,0:T(2,128)(2,1)} %reshape.156), calls=%async_computation | async-start | bytes 262144 | tf_op jit(solution)/shard_map/all_to_all | solution.py:27
  73.6 6.3 %copy-start.15 = (f32[128]{0:T(128)S(1)}, f32[128]{0:T(128)}, u32[]{:S(2)}) copy-start(f32[128]{0:T(128)} %param.15) | copy-start | bytes 1540
  89.7 90.3 %copy-start.4 = (bf16[32,6144]{0,1:T(8,128)(2,1)S(1)}, bf16[32,6144]{0,1:T(8,128)(2,1)}, u32[]{:S(2)}) copy-start(bf16[32,6144]{0,1:T(8,128)(2,1)} %copy-done.3) | copy-start | bytes 1179652
  89.7 90.3 %copy-start.11 = (f32[6144]{0:T(1024)S(1)}, f32[6144]{0:T(1024)}, u32[]{:S(2)}) copy-start(f32[6144]{0:T(1024)} %param.14) | copy-start | bytes 73732
  180.0 11.9 %copy-start.14 = (s32[2]{0:T(128)S(1)}, s32[2]{0:T(128)}, u32[]{:S(2)}) copy-start(s32[2]{0:T(128)} %param.21) | copy-start | bytes 28
  180.0 13.8 %copy-start.12 = (bf16[32,512]{1,0:T(8,128)(2,1)S(1)}, bf16[32,512]{1,0:T(8,128)(2,1)}, u32[]{:S(2)}) copy-start(bf16[32,512]{1,0:T(8,128)(2,1)} %param.20) | copy-start | bytes 98308
  182.4 20.6 %copy-start.1 = (bf16[32,6144]{0,1:T(8,128)(2,1)}, bf16[32,6144]{0,1:T(8,128)(2,1)S(1)}, u32[]{:S(2)}) copy-start(bf16[32,6144]{0,1:T(8,128)(2,1)S(1)} %fusion.4) | copy-start | bytes 1179652
  186.5 16.0 %all-to-all-start.1 = ((bf16[32,2,1024]{2,1,0:T(2,128)(2,1)}), bf16[32,2,1024]{2,1,0:T(2,128)(2,1)S(1)}, u32[]{:S(2)}, u32[]{:S(2)}) async-start(bf16[32,2,1024]{2,1,0:T(2,128)(2,1)} %reshape.158), calls=%async_computation.1 | async-start | bytes 262144 | tf_op jit(solution)/shard_map/all_to_all | solution.py:27
  191.8 158.4 %all-reduce.5.cloned.1.call-start = ((), (), s32[]{:S(2)}) async-start(), calls=%async_computation.3 | async-start | bytes 131072 | tf_op jit(solution)/shard_map/psum | solution.py:12
  194.4 294.6 %all-reduce.7.cloned.1.call-start = ((), (), s32[]{:S(2)}) async-start(), calls=%async_computation.4 | async-start | bytes 6291456 | tf_op jit(solution)/shard_map/psum | solution.py:12
  253.9 90.3 %copy-start.2 = (bf16[32,6144]{0,1:T(8,128)(2,1)S(1)}, bf16[32,6144]{0,1:T(8,128)(2,1)}, u32[]{:S(2)}) copy-start(bf16[32,6144]{0,1:T(8,128)(2,1)} %copy-done.1) | copy-start | bytes 1179652
  253.9 90.3 %copy-start.5 = (bf16[32,6144]{0,1:T(8,128)(2,1)S(1)}, bf16[32,6144]{0,1:T(8,128)(2,1)}, u32[]{:S(2)}) copy-start(bf16[32,6144]{0,1:T(8,128)(2,1)} %copy-done.3) | copy-start | bytes 1179652
  347.7 1.2 copy-start.6
  489.1 2.3 copy-start.8
  489.1 8.8 %copy-start.7 = (bf16[32,6144]{0,1:T(8,128)(2,1)S(1)}, bf16[32,6144]{0,1:T(8,128)(2,1)}, u32[]{:S(2)}) copy-start(bf16[32,6144]{0,1:T(8,128)(2,1)} %copy-done.6) | copy-start | bytes 1179652
  493.6 83.9 %all-to-all-start.2 = ((bf16[32,16,384]{2,0,1:T(8,128)(2,1)}), bf16[32,16,384]{2,0,1:T(8,128)(2,1)}, u32[]{:S(2)}, u32[]{:S(2)}) async-start(bf16[32,16,384]{2,0,1:T(8,128)(2,1)} %bitcast.83), calls=%async_computation.2 | async-start | bytes 786432 | tf_op jit(solution)/shard_map/all_to_all | solution.py:89
Sparse Core Ops, SparseCore 0:
  196.2 123.2 all-reduce.4
  350.3 138.7 all-reduce.6
where the time goes:
time: 587 us; the launch traced here: 586 us
  other arithmetic  195 us (33%)
  waiting for transfers between devices  157 us (27%)
  local copies, waits for them, and re-layouts  114 us (19%)
  blocking collectives  75.4 us (13%)
  starting transfers between devices  24 us (4%)
  between operations  15.8 us (3%)
    scatter-add x2, other arithmetic, add_block(): return totals.at[:, cell_map.reshape(-1)].add(product.reshape(count, -1))  181 us
    psum x2, waiting for transfers between devices, spread(): return lax.psum(jnp.where(mine, value, jnp.zeros_like(value)), axis)  139 us
    gather x4, local copies, waits for them, and re-layouts, add_block(): gathered = jnp.take(extended, cell_map, axis=1)  78.3 us
    psum x1, blocking collectives, per_device(): lax.psum(energy_local, 'mesh') / (node_count * lax.axis_size('mesh'))  75.4 us
    all_to_all x2, starting transfers between devices, import_ghosts(): lax.all_to_all(outgoing, 'mesh', split_axis=1, concat_axis=1, tiled=True)  19.7 us
    all_to_all x2, waiting for transfers between devices, import_ghosts(): lax.all_to_all(outgoing, 'mesh', split_axis=1, concat_axis=1, tiled=True)  18.2 us
    unnamed x41, local copies, waits for them, and re-layouts  13.8 us
  transfers between devices with their start and end apart: 5, of which 3 were waited for; matrix products, arithmetic and copies ran while one was open for 26% of the time, Pallas kernels for 0%

commit v1 on v0

v1 whole, which is shorter than its diff:
```python
import functools

import jax
import jax.numpy as jnp
from jax import lax
from jax.experimental import pallas as pl
from jax.experimental.pallas import tpu as pltpu
from jax.sharding import PartitionSpec as P

center = 6.0
half_width = 4.0
LO = 512
GLO = 128
STEP = 8


def onehot(rows, width):
    level = lax.broadcasted_iota(jnp.int32, (width, 128), 0)
    parts = [jnp.where(level == row, 1.0, 0.0).astype(jnp.bfloat16) for row in rows]
    return jnp.concatenate(parts, axis=1)


def pick(table, indices, count, width):
    shift = width.bit_length() - 1
    rows = [indices[k : k + 1, :] for k in range(indices.shape[0])]
    low = [jnp.bitwise_and(row, width - 1) for row in rows]
    high = [jnp.right_shift(row, shift) for row in rows]
    product = jnp.dot(table, onehot(low, width), preferred_element_type=jnp.float32)
    groups = table.shape[0] // count
    picked = []
    for k in range(len(rows)):
        total = jnp.zeros((count, 128), jnp.float32)
        for group in range(groups):
            part = product[group * count : (group + 1) * count, k * 128 : (k + 1) * 128]
            total = jnp.where(high[k] == group, part, total)
        picked.append(total)
    return picked


def stack_groups(field_ref, table_ref, count, width):
    for group in range(field_ref.shape[1] // width):
        table_ref[group * count : (group + 1) * count, :] = field_ref[
            :, group * width : (group + 1) * width
        ]


def pack_sends(table_ref, send_ref, nbr_ref, out_ref, count):
    out_ref[...] = jnp.zeros(out_ref.shape, out_ref.dtype)
    picked = pick(table_ref[...], send_ref[...], count, LO)
    half = count // 2
    for k, part in enumerate(picked):
        for side in range(2):
            block = part[:, side * 64 : (side + 1) * 64]
            tile = jnp.concatenate([block[:half], block[half:]], axis=1)
            out_ref[nbr_ref[2 * k + side]] = tile.astype(jnp.bfloat16)


def pack_kernel(nbr_ref, field_ref, send_ref, out_ref, table_ref):
    count = field_ref.shape[0]
    stack_groups(field_ref, table_ref, count, LO)
    pack_sends(table_ref, send_ref, nbr_ref, out_ref, count)


def own_kernel(field_ref, index_ref, out_ref, table_ref):
    count = field_ref.shape[0]
    stack_groups(field_ref, table_ref, count, LO)

    def body(step, carry):
        base = pl.multiple_of(step * STEP, STEP)
        picked = pick(table_ref[...], index_ref[pl.ds(base, STEP), :], count, LO)
        for k in range(STEP):
            out_ref[base + k] = picked[k].astype(jnp.bfloat16)
        return carry

    lax.fori_loop(0, index_ref.shape[0] // STEP, body, 0)


def apply_body(
    nbr_ref, field_ref, own_ref, recv_ref, index_ref, ghost_index_ref, kernel_ref,
    scale_ref, ghost_ref, nodes_ref, product_ref, total_ref,
):
    count = field_ref.shape[0]
    half = count // 2
    steps = index_ref.shape[0] // STEP
    for k in range(ghost_ref.shape[0] // count):
        left = recv_ref[nbr_ref[2 * k]]
        right = recv_ref[nbr_ref[2 * k + 1]]
        ghost_ref[k * count : k * count + half, :] = jnp.concatenate(
            [left[:, :64], right[:, :64]], axis=1
        )
        ghost_ref[k * count + half : (k + 1) * count, :] = jnp.concatenate(
            [left[:, 64:], right[:, 64:]], axis=1
        )

    def ghosts(step, carry):
        base = pl.multiple_of(step * STEP, STEP)
        picked = pick(ghost_ref[...], ghost_index_ref[pl.ds(base, STEP), :], count, GLO)
        for k in range(STEP):
            nodes_ref[base + k] = picked[k] + own_ref[base + k].astype(jnp.float32)
        return carry

    lax.fori_loop(0, steps, ghosts, 0)

    for state in range(count):
        columns = nodes_ref[:, state, :].astype(jnp.bfloat16)
        product = jnp.dot(kernel_ref[...], columns, preferred_element_type=jnp.float32)
        product_ref[:, state, :] = product * scale_ref[...]

    total_ref[...] = jnp.zeros(total_ref.shape, jnp.float32)
    groups = total_ref.shape[0] // count
    zero = jnp.zeros((count, 128), jnp.bfloat16)

    def scatter(step, carry):
        base = pl.multiple_of(step * STEP, STEP)
        indices = index_ref[pl.ds(base, STEP), :]
        rows = [indices[k : k + 1, :] for k in range(STEP)]
        low = [jnp.bitwise_and(row, LO - 1) for row in rows]
        high = [jnp.right_shift(row, LO.bit_length() - 1) for row in rows]
        parts = []
        for k in range(STEP):
            value = product_ref[base + k].astype(jnp.float32)
            parts.append(
                jnp.concatenate(
                    [
                        jnp.where(high[k] == group, value, 0.0).astype(jnp.bfloat16)
                        for group in range(groups)
                    ],
                    axis=0,
                )
            )
        left = jnp.concatenate(parts, axis=1)
        total_ref[...] += lax.dot_general(
            left, onehot(low, LO), (((1,), (1,)), ((), ())), preferred_element_type=jnp.float32
        )
        return carry

    lax.fori_loop(0, steps, scatter, 0)


def first_kernel(
    nbr_ref, field_ref, own_ref, recv_ref, index_ref, ghost_index_ref, kernel_ref, scale_ref,
    pot_ref, send_ref, next_ref, out_ref, table_ref, ghost_ref, nodes_ref, product_ref, total_ref,
):
    apply_body(
        nbr_ref, field_ref, own_ref, recv_ref, index_ref, ghost_index_ref, kernel_ref,
        scale_ref, ghost_ref, nodes_ref, product_ref, total_ref,
    )
    count = field_ref.shape[0]
    for group in range(field_ref.shape[1] // LO):
        lanes = slice(group * LO, (group + 1) * LO)
        rows = slice(group * count, (group + 1) * count)
        start = field_ref[:, lanes].astype(jnp.float32)
        image = total_ref[rows, :] + pot_ref[:, lanes] * start
        field = ((image - center * start) / half_width).astype(jnp.bfloat16)
        next_ref[:, lanes] = field
        table_ref[rows, :] = field
    pack_sends(table_ref, send_ref, nbr_ref, out_ref, count)


def second_kernel(
    nbr_ref, field_ref, own_ref, recv_ref, index_ref, ghost_index_ref, kernel_ref, scale_ref,
    pot_ref, start_ref, next_ref, energy_ref, ghost_ref, nodes_ref, product_ref, total_ref,
):
    apply_body(
        nbr_ref, field_ref, own_ref, recv_ref, index_ref, ghost_index_ref, kernel_ref,
        scale_ref, ghost_ref, nodes_ref, product_ref, total_ref,
    )
    count = field_ref.shape[0]
    energy = jnp.zeros((count, LO), jnp.float32)
    for group in range(field_ref.shape[1] // LO):
        lanes = slice(group * LO, (group + 1) * LO)
        rows = slice(group * count, (group + 1) * count)
        one = field_ref[:, lanes].astype(jnp.float32)
        start = start_ref[:, lanes].astype(jnp.float32)
        image = total_ref[rows, :] + pot_ref[:, lanes] * one
        energy = energy + one * image
        next_ref[:, lanes] = (
            2.0 * (image - center * one) / half_width - start
        ).astype(jnp.bfloat16)
    total = energy[:, :128]
    for part in range(1, LO // 128):
        total = total + energy[:, part * 128 : (part + 1) * 128]
    energy_ref[...] = total


vmem = pl.BlockSpec(memory_space=pltpu.VMEM)
smem = pl.BlockSpec(memory_space=pltpu.SMEM)
params = pltpu.CompilerParams(vmem_limit_bytes=48 << 20)


def shape(dims, kind):
    return jax.ShapeDtypeStruct(dims, kind)


def pack(neighbours, field, sends):
    count, nodes = field.shape
    return pl.pallas_call(
        pack_kernel,
        out_shape=shape((lax.axis_size("mesh"), count // 2, 128), jnp.bfloat16),
        in_specs=[smem, vmem, vmem],
        out_specs=vmem,
        scratch_shapes=[pltpu.VMEM((nodes // LO * count, LO), jnp.bfloat16)],
        compiler_params=params,
        name="pack",
    )(neighbours, field, sends)


def gather_own(field, index):
    count, nodes = field.shape
    return pl.pallas_call(
        own_kernel,
        out_shape=shape((index.shape[0], count, 128), jnp.bfloat16),
        in_specs=[vmem, vmem],
        out_specs=vmem,
        scratch_shapes=[pltpu.VMEM((nodes // LO * count, LO), jnp.bfloat16)],
        compiler_params=params,
        name="gather_own",
    )(field, index)


def apply_scratch(count, nodes, index, slots):
    return [
        pltpu.VMEM((slots // GLO * count, GLO), jnp.bfloat16),
        pltpu.VMEM((index.shape[0], count, 128), jnp.float32),
        pltpu.VMEM((index.shape[0], count, 128), jnp.float32),
        pltpu.VMEM((nodes // LO * count, LO), jnp.float32),
    ]


def first(neighbours, field, own, received, index, ghost_index, kernel, scale, pot, sends):
    count, nodes = field.shape
    return pl.pallas_call(
        first_kernel,
        out_shape=(
            shape(field.shape, jnp.bfloat16),
            shape((lax.axis_size("mesh"), count // 2, 128), jnp.bfloat16),
        ),
        in_specs=[smem] + [vmem] * 9,
        out_specs=(vmem, vmem),
        scratch_shapes=[pltpu.VMEM((nodes // LO * count, LO), jnp.bfloat16)]
        + apply_scratch(count, nodes, index, sends.size),
        compiler_params=params,
        name="first",
    )(neighbours, field, own, received, index, ghost_index, kernel, scale, pot, sends)


def second(neighbours, field, own, received, index, ghost_index, kernel, scale, pot, start, slots):
    count, nodes = field.shape
    return pl.pallas_call(
        second_kernel,
        out_shape=(shape(field.shape, jnp.bfloat16), shape((count, 128), jnp.float32)),
        in_specs=[smem] + [vmem] * 9,
        out_specs=(vmem, vmem),
        scratch_shapes=apply_scratch(count, nodes, index, slots),
        compiler_params=params,
        name="second",
    )(neighbours, field, own, received, index, ghost_index, kernel, scale, pot, start)


def swap(value, axis):
    return lax.all_to_all(value, axis, split_axis=0, concat_axis=0, tiled=True)


def prepare(cell_map, neighbours, nodes, slot_count):
    npe, cells = cell_map.shape
    pad = -npe % STEP
    owner = (cell_map - nodes) // slot_count
    position = jnp.zeros_like(cell_map)
    for place in range(neighbours.shape[0]):
        position = jnp.where(owner == neighbours[place], place, position)
    ghost = position * slot_count + (cell_map - nodes) % slot_count
    own = cell_map < nodes
    own_index = jnp.where(own, cell_map, -1)
    ghost_index = jnp.where(own, -1, ghost)
    fill = ((0, pad), (0, 0))
    return (
        jnp.pad(own_index, fill, constant_values=-1),
        jnp.pad(ghost_index, fill, constant_values=-1),
    )


def per_device(
    filter_block,
    local_pot,
    cell_scale,
    cell_kernel,
    cell_map,
    neighbour_ids,
    send_nodes,
    rotation_rows,
    panel_owner,
):
    count, node_count = filter_block.shape
    mesh_size = lax.axis_size("mesh")
    band_size = lax.axis_size("band")
    neighbours = neighbour_ids[0]
    slots = send_nodes.shape[2]
    sends = send_nodes.reshape(-1, 128)
    pot = local_pot.reshape(1, -1)
    scale = cell_scale.reshape(1, -1)
    outgoing = pack(neighbours, filter_block, sends)
    incoming = swap(outgoing, "mesh")
    all_rows = swap(jnp.broadcast_to(rotation_rows, (band_size,) + rotation_rows.shape), "band")
    index, ghost_index = prepare(cell_map, neighbours, node_count, slots)
    pad = index.shape[0] - cell_kernel.shape[0]
    kernel = jnp.pad(cell_kernel, ((0, pad), (0, pad)))
    own = gather_own(filter_block, index)
    field_one, outgoing = first(
        neighbours, filter_block, own, incoming, index, ghost_index, kernel, scale, pot, sends
    )
    incoming = swap(outgoing, "mesh")
    own = gather_own(field_one, index)
    filtered, energy = second(
        neighbours, field_one, own, incoming, index, ghost_index, kernel, scale, pot,
        filter_block, sends.size,
    )
    width = node_count // band_size
    parts = filtered.reshape(count, band_size, width).transpose(1, 0, 2)
    states = swap(parts, "band")
    energy_local = jnp.sum(energy, axis=1)
    gathered = swap(jnp.broadcast_to(energy_local, (mesh_size, 1, count)), "mesh")
    state_energy = jnp.sum(gathered[:, 0, :], axis=0) / (node_count * mesh_size)
    panels = jnp.take(states, panel_owner, axis=0).reshape(-1, width)
    coefficients = jnp.take(all_rows, panel_owner, axis=0).reshape(-1, rotation_rows.shape[1])
    rotated = lax.dot_general(
        coefficients, panels, (((0,), (0,)), ((), ())), preferred_element_type=jnp.float32
    ).astype(jnp.bfloat16)
    return (filtered, rotated, state_energy)


def solution(mesh):
    placed = (
        P("band", "mesh"),
        P("mesh"),
        P("mesh"),
        P(),
        P(None, "mesh"),
        P("mesh", None),
        P("mesh", None, None),
        P("band", None),
        P(),
    )
    return jax.shard_map(
        per_device,
        mesh=mesh,
        in_specs=placed,
        out_specs=(P("band", "mesh"), P(None, ("mesh", "band")), P("band")),
        check_vma=False,
    )
```

time: 587 us -> 160 us (0.27)
  the two profiles are of different devices: /device:TPU:1 before, /device:TPU:10 now
where the time goes in v1:
time: 160 us; the launch traced here: 159 us
  Pallas kernels  60.4 us (38%)
  starting transfers between devices  36.2 us (23%)
  waiting for transfers between devices  27.1 us (17%)
  blocking collectives  17.4 us (11%)
  other arithmetic  9.6 us (6%)
  local copies, waits for them, and re-layouts  6.67 us (4%)
    all_to_all x4, starting transfers between devices, swap(): return lax.all_to_all(value, axis, split_axis=0, concat_axis=0, tiled=True)  36.2 us
    all_to_all x4, waiting for transfers between devices, swap(): return lax.all_to_all(value, axis, split_axis=0, concat_axis=0, tiled=True)  27.1 us
    pallas_call x2, Pallas kernels, gather_own(): pl.pallas_call(own_kernel, out_shape=shape((index.shape[0], count, 128),...  19.6 us
    pallas_call x1, Pallas kernels, first(): pl.pallas_call(first_kernel, out_shape=(shape(field.shape, jnp.bfloat16),...  19.6 us
    pallas_call x1, Pallas kernels, second(): pl.pallas_call(second_kernel, out_shape=(shape(field.shape, jnp.bfloat16)...  19.3 us
    all_to_all x1, blocking collectives, swap(): return lax.all_to_all(value, axis, split_axis=0, concat_axis=0, tiled=True)  17.4 us
    select_n x1, other arithmetic, prepare(): ghost_index = jnp.where(own, -1, ghost)  8.22 us
  transfers between devices with their start and end apart: 4, of which 3 were waited for; matrix products, arithmetic and copies ran while one was open for 7% of the time, Pallas kernels for 12%

profile of v1, /device:TPU:10, one launch (start us, length us, event | category | flops | bytes accessed | tf_op | source)
XLA Modules:
  0.0 159.3 jit_solution(5586093564253388683)
XLA Ops:
  0.6 0.7 reduce.1
  1.4 0.1 reshape.53.send_ref
  1.4 0.7 copy-done.2
  2.1 1.0 copy-done
  3.1 1.9 %pack.1 = bf16[32,16,128]{2,1,0:T(8,128)(2,1)} custom-call(s32[14]{0:T(128)S(1)} %bitcast.28, bf16[32,6144]{1,0:T(8,128)(2,1)S(1)} %copy-done, s32[7,128]{1,0:T(8,128)S(1)} %reshape.53.send_ref), custom_call_target="tpu_custom_call" | custom-call | tf_op jit(solution)/shard_map/pack/pallas_call | solution.py:197
  4.9 12.4 %all-to-all-start = ((bf16[32,16,128]{2,1,0:T(8,128)(2,1)}), bf16[32,16,128]{2,1,0:T(8,128)(2,1)S(1)}, u32[]{:S(2)}, u32[]{:S(2)}) async-start(bf16[32,16,128]{2,1,0:T(8,128)(2,1)} %pack.1), calls=%async_computation | async-start | bytes 262144 | tf_op jit(solution)/shard_map/all_to_all | solution.py:261
  17.3 0.7 fusion.10
  18.0 8.2 %compare_select_fusion = (s32[125,128]{1,0:T(8,128)S(1)}, s32[125,128]{1,0:T(8,128)S(1)}) fusion(s32[125,128]{1,0:T(8,128)S(1)} %copy-done.6, s32[]{:T(128)} %bitcast.13, s32[]{:T(128)} %bitcast.12, s32[]{:T(128)} %bitcast.11, s32[]{:T(128)} %bitcast.10, s32[]{:T(128)} %bitcast.9, s32[]{:T(128)} %bitcast.8, s32[]{:T(128)} %bitcast.7, s32[]{:T(128)} %bitcast.6, ...), kind=kLoop, calls=%fused_computation.10 | loop fusion | flops 816000 | bytes 192052 | tf_op jit(solution)/shard_map/jit(_where)/select_n | solution.py:274
  26.3 0.0 copy-done.1
  26.3 9.9 %gather_own.2.own_ref = bf16[128,32,128]{2,1,0:T(8,128)(2,1)S(1)} custom-call(bf16[32,6144]{1,0:T(8,128)(2,1)S(1)} %copy-done.1, s32[128,128]{1,0:T(8,128)S(1)} %pad.11.index_ref), custom_call_target="tpu_custom_call" | custom-call | tf_op jit(solution)/shard_map/gather_own/pallas_call | solution.py:210
  36.2 0.0 copy-start.8
  36.2 0.7 copy-done.8
  36.9 0.0 all-to-all-done.recv_ref
  36.9 0.0 copy-start.4
  37.0 0.7 copy-done.3
  37.7 19.6 %first.1 = (bf16[32,6144]{1,0:T(8,128)(2,1)S(1)}, bf16[32,16,128]{2,1,0:T(8,128)(2,1)}) custom-call(s32[14]{0:T(128)S(1)} %bitcast.29, bf16[32,6144]{1,0:T(8,128)(2,1)S(1)} %copy-done.1, bf16[128,32,128]{2,1,0:T(8,128)(2,1)S(1)} %gather_own.2.own_ref, bf16[32,16,128]{2,1,0:T(8,128)(2,1)S(1)} %all-to-all-done.recv_ref, s32[128,128]{1,0:T(8,128)S(1)} %pad.11.index_ref, ...), custom_call_target="tpu_custom_call" | custom-call | tf_op jit(solution)/shard_map/first/pallas_call | solution.py:232
  57.3 9.9 %all-to-all-start.1 = ((bf16[32,16,128]{2,1,0:T(8,128)(2,1)}), bf16[32,16,128]{2,1,0:T(8,128)(2,1)S(1)}, u32[]{:S(2)}, u32[]{:S(2)}) async-start(bf16[32,16,128]{2,1,0:T(8,128)(2,1)} %get-tuple-element.8), calls=%async_computation.1 | async-start | bytes 262144 | tf_op jit(solution)/shard_map/all_to_all | solution.py:261
  67.2 9.8 %gather_own.3.own_ref = bf16[128,32,128]{2,1,0:T(8,128)(2,1)S(1)} custom-call(bf16[32,6144]{1,0:T(8,128)(2,1)S(1)} %get-tuple-element.7.field_ref, s32[128,128]{1,0:T(8,128)S(1)} %pad.11.index_ref), custom_call_target="tpu_custom_call" | custom-call | tf_op jit(solution)/shard_map/gather_own/pallas_call | solution.py:210
  77.0 2.0 %all-to-all-done.1.recv_ref = bf16[32,16,128]{2,1,0:T(8,128)(2,1)S(1)} async-done(((bf16[32,16,128]{2,1,0:T(8,128)(2,1)}), bf16[32,16,128]{2,1,0:T(8,128)(2,1)S(1)}, u32[]{:S(2)}, u32[]{:S(2)}) %all-to-all-start.1) | async-done | bytes 131104 | tf_op jit(solution)/shard_map/all_to_all | solution.py:261
  79.0 19.3 %second.1 = (bf16[32,6144]{1,0:T(8,128)(2,1)}, f32[32,128]{1,0:T(8,128)S(1)}) custom-call(s32[14]{0:T(128)S(1)} %bitcast.30, bf16[32,6144]{1,0:T(8,128)(2,1)S(1)} %get-tuple-element.7.field_ref, bf16[128,32,128]{2,1,0:T(8,128)(2,1)S(1)} %gather_own.3.own_ref, bf16[32,16,128]{2,1,0:T(8,128)(2,1)S(1)} %all-to-all-done.1.recv_ref, ...), custom_call_target="tpu_custom_call" | custom-call | tf_op jit(solution)/shard_map/second/pallas_call | solution.py:249
  98.3 0.1 reduce_sum.18
  98.5 17.4 %all_to_all.25 = f32[32,1,32]{2,1,0:T(1,128)S(1)} all-to-all(f32[32,1,32]{2,1,0:T(1,128)S(1)} %broadcast_in_dim.89), channel_id=1, replica_groups=mesh['mesh'=32,'band'=16] {'mesh'}, dimensions={0} | all-to-all | bytes 8192 | tf_op jit(solution)/shard_map/all_to_all | solution.py:261
  115.9 0.8 broadcast_in_dim.84
  116.8 8.7 %all-to-all-start.2 = ((bf16[16,32,512]{2,1,0:T(8,128)(2,1)}), bf16[16,32,512]{2,1,0:T(8,128)(2,1)S(1)}, u32[]{:S(2)}, u32[]{:S(2)}) async-start(bf16[16,32,512]{2,1,0:T(8,128)(2,1)} %broadcast_in_dim.84), calls=%async_computation.2 | async-start | bytes 1048576 | tf_op jit(solution)/shard_map/all_to_all | solution.py:261
  125.4 0.8 copy.18
  126.2 14.3 %all-to-all-done.2 = bf16[16,32,512]{2,1,0:T(8,128)(2,1)S(1)} async-done(((bf16[16,32,512]{2,1,0:T(8,128)(2,1)}), bf16[16,32,512]{2,1,0:T(8,128)(2,1)S(1)}, u32[]{:S(2)}, u32[]{:S(2)}) %all-to-all-start.2) | async-done | bytes 524320 | tf_op jit(solution)/shard_map/all_to_all | solution.py:261
  140.5 5.2 %all-to-all-start.3 = ((bf16[16,32,384]{2,1,0:T(8,128)(2,1)}), bf16[16,32,384]{2,1,0:T(8,128)(2,1)S(1)}, u32[]{:S(2)}, u32[]{:S(2)}) async-start(bf16[16,32,384]{2,1,0:T(8,128)(2,1)} %bitcast.27), calls=%async_computation.3 | async-start | bytes 786432 | tf_op jit(solution)/shard_map/all_to_all | solution.py:261
  145.7 0.5 broadcast_multiply_fusion
  146.3 0.5 gather_fusion
  146.8 10.8 %all-to-all-done.3 = bf16[16,32,384]{2,1,0:T(8,128)(2,1)S(1)} async-done(((bf16[16,32,384]{2,1,0:T(8,128)(2,1)}), bf16[16,32,384]{2,1,0:T(8,128)(2,1)S(1)}, u32[]{:S(2)}, u32[]{:S(2)}) %all-to-all-start.3) | async-done | bytes 393248 | tf_op jit(solution)/shard_map/all_to_all | solution.py:261
  157.6 0.6 gather_fusion.1
  158.2 1.1 fusion
  (21 shorter events, 0.1 us)
Async XLA Ops:
  1.4 0.7 copy-start.2
  2.1 1.0 copy-start
  3.1 15.0 %copy-start.6 = (s32[125,128]{1,0:T(8,128)S(1)}, s32[125,128]{1,0:T(8,128)}, u32[]{:S(2)}) copy-start(s32[125,128]{1,0:T(8,128)} %param.13) | copy-start | bytes 192004
  4.9 21.4 %copy-start.1 = (bf16[32,6144]{1,0:T(8,128)(2,1)S(1)}, bf16[32,6144]{1,0:T(8,128)(2,1)}, u32[]{:S(2)}) copy-start(bf16[32,6144]{1,0:T(8,128)(2,1)} %start_ref.1) | copy-start | bytes 1179652
  4.9 32.0 %all-to-all-start = ((bf16[32,16,128]{2,1,0:T(8,128)(2,1)}), bf16[32,16,128]{2,1,0:T(8,128)(2,1)S(1)}, u32[]{:S(2)}, u32[]{:S(2)}) async-start(bf16[32,16,128]{2,1,0:T(8,128)(2,1)} %pack.1), calls=%async_computation | async-start | bytes 262144 | tf_op jit(solution)/shard_map/all_to_all | solution.py:261
  36.2 0.8 copy-start.8
  36.9 0.7 copy-start.3
  36.9 0.7 copy-start.4
  57.3 21.7 %all-to-all-start.1 = ((bf16[32,16,128]{2,1,0:T(8,128)(2,1)}), bf16[32,16,128]{2,1,0:T(8,128)(2,1)S(1)}, u32[]{:S(2)}, u32[]{:S(2)}) async-start(bf16[32,16,128]{2,1,0:T(8,128)(2,1)} %get-tuple-element.8), calls=%async_computation.1 | async-start | bytes 262144 | tf_op jit(solution)/shard_map/all_to_all | solution.py:261
  98.3 17.6 %copy-start.7 = (bf16[32,512]{1,0:T(8,128)(2,1)S(1)}, bf16[32,512]{1,0:T(8,128)(2,1)}, u32[]{:S(2)}) copy-start(bf16[32,512]{1,0:T(8,128)(2,1)} %param.16) | copy-start | bytes 98308
  116.7 8.7 %copy-start.5 = (bf16[32,6144]{1,0:T(8,128)(2,1)S(1)}, bf16[32,6144]{1,0:T(8,128)(2,1)}, u32[]{:S(2)}) copy-start(bf16[32,6144]{1,0:T(8,128)(2,1)} %get-tuple-element.4) | copy-start | bytes 1179652
  116.8 23.8 %all-to-all-start.2 = ((bf16[16,32,512]{2,1,0:T(8,128)(2,1)}), bf16[16,32,512]{2,1,0:T(8,128)(2,1)S(1)}, u32[]{:S(2)}, u32[]{:S(2)}) async-start(bf16[16,32,512]{2,1,0:T(8,128)(2,1)} %broadcast_in_dim.84), calls=%async_computation.2 | async-start | bytes 1048576 | tf_op jit(solution)/shard_map/all_to_all | solution.py:261
  140.5 5.2 %copy-start.9 = (s32[2]{0:T(128)S(1)}, s32[2]{0:T(128)}, u32[]{:S(2)}) copy-start(s32[2]{0:T(128)} %param.17) | copy-start | bytes 28
  140.5 17.1 %all-to-all-start.3 = ((bf16[16,32,384]{2,1,0:T(8,128)(2,1)}), bf16[16,32,384]{2,1,0:T(8,128)(2,1)S(1)}, u32[]{:S(2)}, u32[]{:S(2)}) async-start(bf16[16,32,384]{2,1,0:T(8,128)(2,1)} %bitcast.27), calls=%async_computation.3 | async-start | bytes 786432 | tf_op jit(solution)/shard_map/all_to_all | solution.py:261

commit v2 on v0

v2 whole, which is shorter than its diff:
```python
import jax
import jax.numpy as jnp
from jax import lax
from jax.experimental import pallas as pl
from jax.experimental.pallas import tpu as pltpu
from jax.sharding import PartitionSpec as P

center = 6.0
half_width = 4.0
LO = 512
GLO = 128
STEP = 8


def chunks(total):
    return [(base, min(STEP, total - base)) for base in range(0, total, STEP)]


def flags(row, width):
    parts = []
    level = lax.broadcasted_iota(jnp.int32, (min(width, 256), 128), 0)
    level = level.astype(jnp.float32).astype(jnp.bfloat16)
    one = jnp.ones(level.shape, jnp.bfloat16)
    zero = jnp.zeros(level.shape, jnp.bfloat16)
    for base in range(0, width, level.shape[0]):
        local = row - base
        local = jnp.where((local >= 0) & (local < level.shape[0]), local, -1)
        local = local.astype(jnp.float32).astype(jnp.bfloat16)
        parts.append(jnp.where(level == jnp.broadcast_to(local, level.shape), one, zero))
    return parts[0] if len(parts) == 1 else jnp.concatenate(parts, axis=0)


def low_part(row, width):
    return jnp.bitwise_and(row, width - 1)


def high_part(row, width):
    return jnp.right_shift(row, width.bit_length() - 1)


def choose(product, highs, count):
    groups = product.shape[0] // count
    picked = []
    for k, high in enumerate(highs):
        total = jnp.zeros((count, 128), jnp.float32)
        for group in range(groups):
            part = product[group * count : (group + 1) * count, k * 128 : (k + 1) * 128]
            total = jnp.where(high == group, part, total)
        picked.append(total)
    return picked


def row_list(block):
    return [block[k : k + 1, :] for k in range(block.shape[0])]


def stack_groups(field_ref, table_ref, count):
    for group in range(field_ref.shape[1] // LO):
        table_ref[group * count : (group + 1) * count, :] = field_ref[
            :, group * LO : (group + 1) * LO
        ]


def pack_sends(table_ref, send_ref, nbr_ref, out_ref, count):
    out_ref[...] = jnp.zeros(out_ref.shape, out_ref.dtype)
    rows = row_list(send_ref[...])
    marks = jnp.concatenate([flags(low_part(row, LO), LO) for row in rows], axis=1)
    product = jnp.dot(table_ref[...], marks, preferred_element_type=jnp.float32)
    picked = choose(product, [high_part(row, LO) for row in rows], count)
    half = count // 2
    for k, part in enumerate(picked):
        for side in range(2):
            block = part[:, side * 64 : (side + 1) * 64]
            tile = jnp.concatenate([block[:half], block[half:]], axis=1)
            out_ref[nbr_ref[2 * k + side]] = tile.astype(jnp.bfloat16)


def pack_kernel(nbr_ref, field_ref, send_ref, out_ref, table_ref):
    count = field_ref.shape[0]
    stack_groups(field_ref, table_ref, count)
    pack_sends(table_ref, send_ref, nbr_ref, out_ref, count)


def gather_chunk(table, map_ref, marks, own_ref, base, size, count):
    product = jnp.dot(table, marks, preferred_element_type=jnp.float32)
    rows = row_list(map_ref[base : base + size, :])
    for k, part in enumerate(choose(product, [high_part(row, LO) for row in rows], count)):
        own_ref[base + k] = part.astype(jnp.bfloat16)


def build_kernel(nbr_ref, field_ref, map_ref, own_ref, mark_ref, ghost_mark_ref, high_ref, table_ref):
    count, nodes = field_ref.shape
    stack_groups(field_ref, table_ref, count)
    for base, size in chunks(map_ref.shape[0]):
        block = map_ref[base : base + size, :]
        marks = jnp.concatenate([flags(low_part(row, LO), LO) for row in row_list(block)], axis=1)
        lanes = slice(base * 128, (base + size) * 128)
        mark_ref[:, lanes] = marks
        gather_chunk(table_ref[...], map_ref, marks, own_ref, base, size, count)
        slot = block - nodes
        owner = jnp.right_shift(slot, 6)
        place = jnp.full(block.shape, -1, jnp.int32)
        for position in range(nbr_ref.shape[0]):
            place = jnp.where(owner == nbr_ref[position], position, place)
        compact = jnp.where(place >= 0, place * 64 + jnp.bitwise_and(slot, 63), -1)
        high_ref[base : base + size, :] = high_part(compact, GLO)
        ghost_mark_ref[:, lanes] = jnp.concatenate(
            [flags(low_part(row, GLO), GLO) for row in row_list(compact)], axis=1
        )


def gather_kernel(field_ref, map_ref, mark_ref, own_ref, table_ref):
    count = field_ref.shape[0]
    stack_groups(field_ref, table_ref, count)
    for base, size in chunks(map_ref.shape[0]):
        marks = mark_ref[:, base * 128 : (base + size) * 128]
        gather_chunk(table_ref[...], map_ref, marks, own_ref, base, size, count)


def contract(
    nbr_ref, own_ref, recv_ref, high_ref, ghost_mark_ref, kernel_ref, scale_ref,
    ghost_ref, square_ref, nodes_ref, product_ref,
):
    npe, count, _ = own_ref.shape
    half = count // 2
    for k in range(ghost_ref.shape[0] // count):
        left = recv_ref[nbr_ref[2 * k]]
        right = recv_ref[nbr_ref[2 * k + 1]]
        ghost_ref[k * count : k * count + half, :] = jnp.concatenate(
            [left[:, :64], right[:, :64]], axis=1
        )
        ghost_ref[k * count + half : (k + 1) * count, :] = jnp.concatenate(
            [left[:, 64:], right[:, 64:]], axis=1
        )
    for base, size in chunks(npe):
        marks = ghost_mark_ref[:, base * 128 : (base + size) * 128]
        product = jnp.dot(ghost_ref[...], marks, preferred_element_type=jnp.float32)
        rows = row_list(high_ref[base : base + size, :])
        for k, part in enumerate(choose(product, rows, count)):
            nodes_ref[base + k] = part + own_ref[base + k].astype(jnp.float32)
    square_ref[...] = jnp.zeros(square_ref.shape, square_ref.dtype)
    square_ref[:npe, :npe] = kernel_ref[...]
    nodes_ref[npe:] = jnp.zeros((nodes_ref.shape[0] - npe,) + nodes_ref.shape[1:], jnp.float32)
    scale = scale_ref[...]
    for state in range(0, count, 2):
        columns = jnp.concatenate(
            [nodes_ref[:, state, :], nodes_ref[:, state + 1, :]], axis=1
        ).astype(jnp.bfloat16)
        product = jnp.dot(square_ref[...], columns, preferred_element_type=jnp.float32)
        product_ref[:, state, :] = product[:, :128] * scale
        product_ref[:, state + 1, :] = product[:, 128:] * scale


def scatter(map_ref, mark_ref, product_ref, total_ref, count):
    groups = total_ref.shape[0] // count
    zero = jnp.zeros((count, 128), jnp.bfloat16)
    for base, size in chunks(map_ref.shape[0]):
        parts = []
        for k, row in enumerate(row_list(map_ref[base : base + size, :])):
            high = high_part(row, LO).astype(jnp.float32).astype(jnp.bfloat16)
            high = jnp.broadcast_to(high, zero.shape)
            value = product_ref[base + k].astype(jnp.bfloat16)
            parts.append(
                jnp.concatenate(
                    [
                        jnp.where(high == jnp.full(zero.shape, group, jnp.bfloat16), value, zero)
                        for group in range(groups)
                    ],
                    axis=0,
                )
            )
        marks = mark_ref[:, base * 128 : (base + size) * 128]
        sums = lax.dot_general(
            jnp.concatenate(parts, axis=1), marks, (((1,), (1,)), ((), ())),
            preferred_element_type=jnp.float32,
        )
        if base == 0:
            total_ref[...] = sums
        else:
            total_ref[...] += sums


def first_kernel(
    nbr_ref, field_ref, own_ref, recv_ref, map_ref, mark_ref, high_ref, ghost_mark_ref,
    kernel_ref, scale_ref, pot_ref, send_ref,
    next_ref, out_ref, table_ref, ghost_ref, square_ref, nodes_ref, product_ref, total_ref,
):
    count = field_ref.shape[0]
    contract(
        nbr_ref, own_ref, recv_ref, high_ref, ghost_mark_ref, kernel_ref, scale_ref,
        ghost_ref, square_ref, nodes_ref, product_ref,
    )
    scatter(map_ref, mark_ref, product_ref, total_ref, count)
    for group in range(field_ref.shape[1] // LO):
        lanes = slice(group * LO, (group + 1) * LO)
        rows = slice(group * count, (group + 1) * count)
        start = field_ref[:, lanes].astype(jnp.float32)
        image = total_ref[rows, :] + pot_ref[:, lanes] * start
        field = ((image - center * start) / half_width).astype(jnp.bfloat16)
        next_ref[:, lanes] = field
        table_ref[rows, :] = field
    pack_sends(table_ref, send_ref, nbr_ref, out_ref, count)


def energy_kernel(
    nbr_ref, field_ref, own_ref, recv_ref, high_ref, ghost_mark_ref, kernel_ref, scale_ref,
    pot_ref, cells_ref, energy_ref, ghost_ref, square_ref, nodes_ref, product_ref,
):
    count, nodes = field_ref.shape
    contract(
        nbr_ref, own_ref, recv_ref, high_ref, ghost_mark_ref, kernel_ref, scale_ref,
        ghost_ref, square_ref, nodes_ref, product_ref,
    )
    total = jnp.zeros((count, 128), jnp.float32)
    for base in range(own_ref.shape[0]):
        value = product_ref[base]
        cells_ref[base] = value.astype(jnp.bfloat16)
        total = total + value * own_ref[base].astype(jnp.float32)
    for base in range(0, nodes, 128):
        one = field_ref[:, base : base + 128].astype(jnp.float32)
        total = total + pot_ref[:, base : base + 128] * one * one
    sums = jnp.broadcast_to(jnp.sum(total, axis=1, keepdims=True), total.shape)
    state = lax.broadcasted_iota(jnp.int32, total.shape, 0)
    lane = lax.broadcasted_iota(jnp.int32, total.shape, 1)
    line = jnp.sum(jnp.where(state == lane, sums, 0.0), axis=0, keepdims=True)
    energy_ref[...] = jnp.broadcast_to(line[None], energy_ref.shape)


def second_kernel(
    field_ref, cells_ref, map_ref, mark_ref, pot_ref, start_ref, next_ref, out_ref, total_ref
):
    count = field_ref.shape[0]
    scatter(map_ref, mark_ref, cells_ref, total_ref, count)
    for group in range(field_ref.shape[1] // LO):
        lanes = slice(group * LO, (group + 1) * LO)
        rows = slice(group * count, (group + 1) * count)
        one = field_ref[:, lanes].astype(jnp.float32)
        start = start_ref[:, lanes].astype(jnp.float32)
        image = total_ref[rows, :] + pot_ref[:, lanes] * one
        next_ref[:, lanes] = (
            2.0 * (image - center * one) / half_width - start
        ).astype(jnp.bfloat16)
    width = out_ref.shape[2]
    for band in range(out_ref.shape[0]):
        out_ref[band] = next_ref[:, band * width : (band + 1) * width]


def rotate_kernel(owner_ref, rows_ref, states_ref, out_ref):
    coefficients = [rows_ref[owner_ref[k]] for k in range(owner_ref.shape[0])]
    panels = [states_ref[owner_ref[k]] for k in range(owner_ref.shape[0])]
    out_ref[...] = lax.dot_general(
        jnp.concatenate(coefficients, axis=0),
        jnp.concatenate(panels, axis=0),
        (((0,), (0,)), ((), ())),
        preferred_element_type=jnp.float32,
    ).astype(jnp.bfloat16)


vmem = pl.BlockSpec(memory_space=pltpu.VMEM)
smem = pl.BlockSpec(memory_space=pltpu.SMEM)


def call(kernel, name, outs, scratch, scalar, *operands):
    return pl.pallas_call(
        kernel,
        out_shape=tuple(jax.ShapeDtypeStruct(dims, kind) for dims, kind in outs),
        in_specs=[smem] * scalar + [vmem] * (len(operands) - scalar),
        out_specs=tuple(vmem for _ in outs),
        scratch_shapes=[pltpu.VMEM(dims, kind) for dims, kind in scratch],
        compiler_params=pltpu.CompilerParams(vmem_limit_bytes=LIMIT),
        name=name,
    )(*operands)


LIMIT = 20 << 20
half = jnp.bfloat16
full = jnp.float32


def swap(value, axis):
    return lax.all_to_all(value, axis, split_axis=0, concat_axis=0, tiled=True)


def per_device(
    filter_block,
    local_pot,
    cell_scale,
    cell_kernel,
    cell_map,
    neighbour_ids,
    send_nodes,
    rotation_rows,
    panel_owner,
):
    count, nodes = filter_block.shape
    npe, cells = cell_map.shape
    mesh_size = lax.axis_size("mesh")
    band_size = lax.axis_size("band")
    neighbours = neighbour_ids[0]
    sends = send_nodes.reshape(-1, 128)
    pot = local_pot.reshape(1, -1)
    scale = cell_scale.reshape(1, -1)
    table = ((nodes // LO * count, LO), half)
    total = ((nodes // LO * count, LO), full)
    outbox = ((mesh_size, count // 2, 128), half)
    columns = ((npe, count, cells), half)
    padded = npe + -npe % 8
    inner = [
        ((send_nodes.size // GLO * count, GLO), half),
        ((padded, padded), half),
        ((padded, count, cells), full),
        ((padded, count, cells), full),
    ]

    (outgoing,) = call(pack_kernel, "pack", [outbox], [table], 1, neighbours, filter_block, sends)
    incoming = swap(outgoing, "mesh")
    own, marks, ghost_marks, highs = call(
        build_kernel, "build",
        [columns, ((LO, npe * cells), half), ((GLO, npe * cells), half), ((npe, cells), jnp.int32)],
        [table], 1, neighbours, filter_block, cell_map,
    )
    field_one, outgoing = call(
        first_kernel, "first", [((count, nodes), half), outbox], [table] + inner + [total], 1,
        neighbours, filter_block, own, incoming, cell_map, marks, highs, ghost_marks,
        cell_kernel, scale, pot, sends,
    )
    incoming = swap(outgoing, "mesh")
    (own,) = call(gather_kernel, "gather", [columns], [table], 0, field_one, cell_map, marks)
    all_rows = swap(jnp.broadcast_to(rotation_rows, (band_size,) + rotation_rows.shape), "band")
    products, energy = call(
        energy_kernel, "energy", [columns, ((mesh_size, 1, 128), full)], inner, 1,
        neighbours, field_one, own, incoming, highs, ghost_marks, cell_kernel, scale, pot,
    )
    energies = swap(energy, "mesh")
    filtered, parts = call(
        second_kernel, "second",
        [((count, nodes), half), ((band_size, count, nodes // band_size), half)], [total], 0,
        field_one, products, cell_map, marks, pot, filter_block,
    )
    parts, all_rows, energies = lax.optimization_barrier((parts, all_rows, energies))
    states = swap(parts, "band")
    state_energy = jnp.sum(energies[:, 0, :count], axis=0) / (nodes * mesh_size)
    (rotated,) = call(
        rotate_kernel, "rotate", [((rotation_rows.shape[1], nodes // band_size), half)], [], 1,
        panel_owner, all_rows, states,
    )
    return (filtered, rotated, state_energy)


def solution(mesh):
    placed = (
        P("band", "mesh"),
        P("mesh"),
        P("mesh"),
        P(),
        P(None, "mesh"),
        P("mesh", None),
        P("mesh", None, None),
        P("band", None),
        P(),
    )
    return jax.shard_map(
        per_device,
        mesh=mesh,
        in_specs=placed,
        out_specs=(P("band", "mesh"), P(None, ("mesh", "band")), P("band")),
        check_vma=False,
    )
```

time: 587 us -> 154 us (0.26)
  the two profiles are of different devices: /device:TPU:1 before, /device:TPU:10 now
where the time goes in v2:
time: 154 us; the launch traced here: 153 us
  Pallas kernels  43.1 us (28%)
  local copies, waits for them, and re-layouts  38.5 us (25%)
  starting transfers between devices  37 us (24%)
  blocking collectives  19.5 us (13%)
  waiting for transfers between devices  13.1 us (9%)
    pallas_call x7, Pallas kernels, call(): pl.pallas_call(kernel, out_shape=tuple((jax.ShapeDtypeStruct(dims, kind)...  43.1 us
    unnamed x52, local copies, waits for them, and re-layouts  37.6 us
    all_to_all x4, starting transfers between devices, swap(): return lax.all_to_all(value, axis, split_axis=0, concat_axis=0, tiled=True)  37 us
    all_to_all x1, blocking collectives, swap(): return lax.all_to_all(value, axis, split_axis=0, concat_axis=0, tiled=True)  19.5 us
    all_to_all x4, waiting for transfers between devices, swap(): return lax.all_to_all(value, axis, split_axis=0, concat_axis=0, tiled=True)  13.1 us
  transfers between devices with their start and end apart: 4, of which 2 were waited for; matrix products, arithmetic and copies ran while one was open for 0% of the time, Pallas kernels for 14%

profile of v2, /device:TPU:10, one launch (start us, length us, event | category | flops | bytes accessed | tf_op | source)
XLA Modules:
  0.0 153.3 jit_solution(18346213550545774173)
XLA Ops:
  0.6 0.7 reduce.1
  1.4 1.0 copy-done.7
  2.4 0.7 copy-done.18
  3.1 1.9 %pack.1 = bf16[32,16,128]{2,1,0:T(8,128)(2,1)} custom-call(s32[14]{0:T(128)S(1)} %bitcast.6, bf16[32,6144]{1,0:T(8,128)(2,1)S(1)} %copy-done.7, s32[7,128]{1,0:T(8,128)S(1)} %reshape.15.send_ref), custom_call_target="tpu_custom_call" | custom-call | tf_op jit(solution)/shard_map/pack/pallas_call | solution.py:264
  4.9 12.3 %all-to-all-start = ((bf16[32,16,128]{2,1,0:T(8,128)(2,1)}), bf16[32,16,128]{2,1,0:T(8,128)(2,1)S(1)}, u32[]{:S(2)}, u32[]{:S(2)}) async-start(bf16[32,16,128]{2,1,0:T(8,128)(2,1)} %pack.1), calls=%async_computation | async-start | bytes 262144 | tf_op jit(solution)/shard_map/all_to_all | solution.py:281
  17.2 1.0 copy-done.8
  18.2 0.8 copy-done.11
  19.0 0.7 copy-done.19
  19.7 7.5 %build.1 = (bf16[125,32,128]{2,1,0:T(8,128)(2,1)S(1)}, bf16[512,16000]{1,0:T(8,128)(2,1)S(1)}, bf16[128,16000]{1,0:T(8,128)(2,1)S(1)}, s32[125,128]{1,0:T(8,128)S(1)}) custom-call(s32[14]{0:T(128)S(1)} %bitcast.7, bf16[32,6144]{1,0:T(8,128)(2,1)S(1)} %copy-done.8, s32[125,128]{1,0:T(8,128)S(1)} %copy-done.11), custom_call_target="tpu_custom_call" | custom-call | tf_op jit(solution)/shard_map/build/pallas_call | solution.py:264
  27.2 5.6 %copy-done = bf16[512,16000]{1,0:T(8,128)(2,1)} copy-done((bf16[512,16000]{1,0:T(8,128)(2,1)}, bf16[512,16000]{1,0:T(8,128)(2,1)S(1)}, u32[]{:S(2)}) %copy-start) | copy-done | bytes 16384024
  32.8 1.9 %copy-done.4 = bf16[128,16000]{1,0:T(8,128)(2,1)} copy-done((bf16[128,16000]{1,0:T(8,128)(2,1)}, bf16[128,16000]{1,0:T(8,128)(2,1)S(1)}, u32[]{:S(2)}) %copy-start.4) | copy-done | bytes 4096024
  34.7 5.7 %copy-done.1 = bf16[512,16000]{1,0:T(8,128)(2,1)S(1)} copy-done((bf16[512,16000]{1,0:T(8,128)(2,1)S(1)}, bf16[512,16000]{1,0:T(8,128)(2,1)}, u32[]{:S(2)}) %copy-start.1) | copy-done | bytes 16384024
  40.4 2.2 %copy-done.5 = bf16[128,16000]{1,0:T(8,128)(2,1)S(1)} copy-done((bf16[128,16000]{1,0:T(8,128)(2,1)S(1)}, bf16[128,16000]{1,0:T(8,128)(2,1)}, u32[]{:S(2)}) %copy-start.5) | copy-done | bytes 4096024
  42.5 1.0 copy-done.9
  43.5 0.8 copy-done.12
  44.4 0.7 copy-done.14
  45.1 0.8 copy-done.16
  47.2 12.9 %first.1 = (bf16[32,6144]{1,0:T(8,128)(2,1)S(1)}, bf16[32,16,128]{2,1,0:T(8,128)(2,1)}) custom-call(s32[14]{0:T(128)S(1)} %bitcast.8, bf16[32,6144]{1,0:T(8,128)(2,1)S(1)} %copy-done.9, bf16[125,32,128]{2,1,0:T(8,128)(2,1)S(1)} %get-tuple-element.16.own_ref, bf16[32,16,128]{2,1,0:T(8,128)(2,1)S(1)} %all-to-all-done.recv_ref, s32[125,128]{1,0:T(8,128)S(1)} %copy-done.12, ...), custom_call_target="tpu_custom_call" | custom-call | tf_op jit(solution)/shard_map/first/pallas_call | solution.py:264
  60.0 9.9 %all-to-all-start.1 = ((bf16[32,16,128]{2,1,0:T(8,128)(2,1)}), bf16[32,16,128]{2,1,0:T(8,128)(2,1)S(1)}, u32[]{:S(2)}, u32[]{:S(2)}) async-start(bf16[32,16,128]{2,1,0:T(8,128)(2,1)} %get-tuple-element.21), calls=%async_computation.1 | async-start | bytes 262144 | tf_op jit(solution)/shard_map/all_to_all | solution.py:281
  70.0 5.6 %copy-done.2 = bf16[512,16000]{1,0:T(8,128)(2,1)S(1)} copy-done((bf16[512,16000]{1,0:T(8,128)(2,1)S(1)}, bf16[512,16000]{1,0:T(8,128)(2,1)}, u32[]{:S(2)}) %copy-start.2) | copy-done | bytes 16384024
  75.7 6.6 %gather.1.own_ref = bf16[125,32,128]{2,1,0:T(8,128)(2,1)S(1)} custom-call(bf16[32,6144]{1,0:T(8,128)(2,1)S(1)} %get-tuple-element.20.field_ref, s32[125,128]{1,0:T(8,128)S(1)} %copy-done.13, bf16[512,16000]{1,0:T(8,128)(2,1)S(1)} %copy-done.2), custom_call_target="tpu_custom_call" | custom-call | tf_op jit(solution)/shard_map/gather/pallas_call | solution.py:264
  82.3 2.2 %copy-done.6 = bf16[128,16000]{1,0:T(8,128)(2,1)S(1)} copy-done((bf16[128,16000]{1,0:T(8,128)(2,1)S(1)}, bf16[128,16000]{1,0:T(8,128)(2,1)}, u32[]{:S(2)}) %copy-start.6) | copy-done | bytes 4096024
  84.5 5.2 %energy.1 = (bf16[125,32,128]{2,1,0:T(8,128)(2,1)S(1)}, f32[32,1,128]{2,1,0:T(1,128)S(1)}) custom-call(s32[14]{0:T(128)S(1)} %bitcast.9, bf16[32,6144]{1,0:T(8,128)(2,1)S(1)} %get-tuple-element.20.field_ref, bf16[125,32,128]{2,1,0:T(8,128)(2,1)S(1)} %gather.1.own_ref, bf16[32,16,128]{2,1,0:T(8,128)(2,1)S(1)} %all-to-all-done.1.recv_ref, ...), custom_call_target="tpu_custom_call" | custom-call | tf_op jit(solution)/shard_map/energy/pallas_call | solution.py:264
  89.7 19.5 %all_to_all.25 = f32[32,1,128]{2,1,0:T(1,128)S(1)} all-to-all(f32[32,1,128]{2,1,0:T(1,128)S(1)} %get-tuple-element.25), channel_id=1, replica_groups=mesh['mesh'=32,'band'=16] {'mesh'}, dimensions={0} | all-to-all | bytes 32768 | tf_op jit(solution)/shard_map/all_to_all | solution.py:281
  109.2 0.9 broadcast_in_dim.3
  110.1 8.5 %all-to-all-start.2 = ((bf16[16,32,512]{2,1,0:T(8,128)(2,1)}), bf16[16,32,512]{2,1,0:T(8,128)(2,1)S(1)}, u32[]{:S(2)}, u32[]{:S(2)}) async-start(bf16[16,32,512]{2,1,0:T(8,128)(2,1)} %broadcast_in_dim.3), calls=%async_computation.2 | async-start | bytes 1048576 | tf_op jit(solution)/shard_map/all_to_all | solution.py:281
  118.5 5.6 %copy-done.3 = bf16[512,16000]{1,0:T(8,128)(2,1)S(1)} copy-done((bf16[512,16000]{1,0:T(8,128)(2,1)S(1)}, bf16[512,16000]{1,0:T(8,128)(2,1)}, u32[]{:S(2)}) %copy-start.3) | copy-done | bytes 16384024
  124.2 7.6 %second.1 = (bf16[32,6144]{1,0:T(8,128)(2,1)}, bf16[16,32,384]{2,1,0:T(8,128)(2,1)}) custom-call(bf16[32,6144]{1,0:T(8,128)(2,1)S(1)} %get-tuple-element.20.field_ref, bf16[125,32,128]{2,1,0:T(8,128)(2,1)S(1)} %get-tuple-element.22.cells_ref, s32[125,128]{1,0:T(8,128)S(1)} %copy-done.13, bf16[512,16000]{1,0:T(8,128)(2,1)S(1)} %copy-done.3, ...), custom_call_target="tpu_custom_call" | custom-call | tf_op jit(solution)/shard_map/second/pallas_call | solution.py:264
  131.8 1.8 %all-to-all-done.2.rows_ref = bf16[16,32,512]{2,1,0:T(8,128)(2,1)S(1)} async-done(((bf16[16,32,512]{2,1,0:T(8,128)(2,1)}), bf16[16,32,512]{2,1,0:T(8,128)(2,1)S(1)}, u32[]{:S(2)}, u32[]{:S(2)}) %all-to-all-start.2) | async-done | bytes 524320 | tf_op jit(solution)/shard_map/all_to_all | solution.py:281
  133.6 6.3 %all-to-all-start.4 = ((bf16[16,32,384]{2,1,0:T(8,128)(2,1)}), bf16[16,32,384]{2,1,0:T(8,128)(2,1)S(1)}, u32[]{:S(2)}, u32[]{:S(2)}) async-start(bf16[16,32,384]{2,1,0:T(8,128)(2,1)} %get-tuple-element.27), calls=%async_computation.4 | async-start | bytes 786432 | tf_op jit(solution)/shard_map/all_to_all | solution.py:281
  140.5 11.2 %all-to-all-done.4.states_ref = bf16[16,32,384]{2,1,0:T(8,128)(2,1)S(1)} async-done(((bf16[16,32,384]{2,1,0:T(8,128)(2,1)}), bf16[16,32,384]{2,1,0:T(8,128)(2,1)S(1)}, u32[]{:S(2)}, u32[]{:S(2)}) %all-to-all-start.4) | async-done | bytes 393248 | tf_op jit(solution)/shard_map/all_to_all | solution.py:281
  151.7 1.6 %rotate.1 = bf16[512,384]{1,0:T(8,128)(2,1)} custom-call(s32[2]{0:T(128)S(1)} %copy-done.24, bf16[16,32,512]{2,1,0:T(8,128)(2,1)S(1)} %all-to-all-done.2.rows_ref, bf16[16,32,384]{2,1,0:T(8,128)(2,1)S(1)} %all-to-all-done.4.states_ref), custom_call_target="tpu_custom_call" | custom-call | tf_op jit(solution)/shard_map/rotate/pallas_call | solution.py:264
  (41 shorter events, 2.0 us)
Async XLA Ops:
  1.4 1.0 copy-start.7
  2.4 0.7 copy-start.18
  3.1 66.9 %copy-start.13 = (s32[125,128]{1,0:T(8,128)S(1)}, s32[125,128]{1,0:T(8,128)}, u32[]{:S(2)}) copy-start(s32[125,128]{1,0:T(8,128)} %map_ref.7) | copy-start | bytes 192004
  4.9 29.8 %all-to-all-start = ((bf16[32,16,128]{2,1,0:T(8,128)(2,1)}), bf16[32,16,128]{2,1,0:T(8,128)(2,1)S(1)}, u32[]{:S(2)}, u32[]{:S(2)}) async-start(bf16[32,16,128]{2,1,0:T(8,128)(2,1)} %pack.1), calls=%async_computation | async-start | bytes 262144 | tf_op jit(solution)/shard_map/all_to_all | solution.py:281
  17.2 1.0 copy-start.8
  18.2 0.8 copy-start.11
  19.0 0.7 copy-start.19
  27.2 5.6 %copy-start = (bf16[512,16000]{1,0:T(8,128)(2,1)}, bf16[512,16000]{1,0:T(8,128)(2,1)S(1)}, u32[]{:S(2)}) copy-start(bf16[512,16000]{1,0:T(8,128)(2,1)S(1)} %get-tuple-element.17.mark_ref) | copy-start | bytes 49152004
  32.8 1.9 %copy-start.4 = (bf16[128,16000]{1,0:T(8,128)(2,1)}, bf16[128,16000]{1,0:T(8,128)(2,1)S(1)}, u32[]{:S(2)}) copy-start(bf16[128,16000]{1,0:T(8,128)(2,1)S(1)} %get-tuple-element.19.ghost_mark_ref) | copy-start | bytes 12288004
  34.7 5.7 %copy-start.1 = (bf16[512,16000]{1,0:T(8,128)(2,1)S(1)}, bf16[512,16000]{1,0:T(8,128)(2,1)}, u32[]{:S(2)}) copy-start(bf16[512,16000]{1,0:T(8,128)(2,1)} %copy-done) | copy-start | bytes 49152004
  40.4 2.2 %copy-start.5 = (bf16[128,16000]{1,0:T(8,128)(2,1)S(1)}, bf16[128,16000]{1,0:T(8,128)(2,1)}, u32[]{:S(2)}) copy-start(bf16[128,16000]{1,0:T(8,128)(2,1)} %copy-done.4) | copy-start | bytes 12288004
  42.5 1.0 copy-start.9
  43.5 0.8 copy-start.12
  44.4 0.7 copy-start.14
  45.1 0.8 copy-start.16
  45.9 0.7 copy-start.20
  46.5 0.7 copy-start.22
  47.2 35.1 %copy-start.15 = (f32[6144]{0:T(1024)S(1)}, f32[6144]{0:T(1024)}, u32[]{:S(2)}) copy-start(f32[6144]{0:T(1024)} %param.10) | copy-start | bytes 73732
  47.2 35.1 %copy-start.17 = (bf16[125,125]{1,0:T(8,128)(2,1)S(1)}, bf16[125,125]{1,0:T(8,128)(2,1)}, u32[]{:S(2)}) copy-start(bf16[125,125]{1,0:T(8,128)(2,1)} %kernel_ref.3) | copy-start | bytes 93754
  47.2 35.1 %copy-start.21 = (s32[1,14]{1,0:T(1,128)S(1)}, s32[1,14]{1,0:T(1,128)}, u32[]{:S(2)}) copy-start(s32[1,14]{1,0:T(1,128)} %param.14) | copy-start | bytes 172
  47.2 35.1 %copy-start.23 = (f32[128]{0:T(128)S(1)}, f32[128]{0:T(128)}, u32[]{:S(2)}) copy-start(f32[128]{0:T(128)} %param.11) | copy-start | bytes 1540
  47.2 71.4 %copy-start.10 = (bf16[32,6144]{1,0:T(8,128)(2,1)S(1)}, bf16[32,6144]{1,0:T(8,128)(2,1)}, u32[]{:S(2)}) copy-start(bf16[32,6144]{1,0:T(8,128)(2,1)} %start_ref.1) | copy-start | bytes 1179652
  60.0 49.1 %copy-start.25 = (bf16[32,512]{1,0:T(8,128)(2,1)S(1)}, bf16[32,512]{1,0:T(8,128)(2,1)}, u32[]{:S(2)}) copy-start(bf16[32,512]{1,0:T(8,128)(2,1)} %param.16) | copy-start | bytes 98308
  60.0 22.2 %all-to-all-start.1 = ((bf16[32,16,128]{2,1,0:T(8,128)(2,1)}), bf16[32,16,128]{2,1,0:T(8,128)(2,1)S(1)}, u32[]{:S(2)}, u32[]{:S(2)}) async-start(bf16[32,16,128]{2,1,0:T(8,128)(2,1)} %get-tuple-element.21), calls=%async_computation.1 | async-start | bytes 262144 | tf_op jit(solution)/shard_map/all_to_all | solution.py:281
  70.0 5.7 %copy-start.2 = (bf16[512,16000]{1,0:T(8,128)(2,1)S(1)}, bf16[512,16000]{1,0:T(8,128)(2,1)}, u32[]{:S(2)}) copy-start(bf16[512,16000]{1,0:T(8,128)(2,1)} %copy-done) | copy-start | bytes 49152004
  82.3 2.2 %copy-start.6 = (bf16[128,16000]{1,0:T(8,128)(2,1)S(1)}, bf16[128,16000]{1,0:T(8,128)(2,1)}, u32[]{:S(2)}) copy-start(bf16[128,16000]{1,0:T(8,128)(2,1)} %copy-done.4) | copy-start | bytes 12288004
  84.5 67.3 %copy-start.24 = (s32[2]{0:T(128)S(1)}, s32[2]{0:T(128)}, u32[]{:S(2)}) copy-start(s32[2]{0:T(128)} %owner_ref.1) | copy-start | bytes 28
  110.1 23.6 %all-to-all-start.2 = ((bf16[16,32,512]{2,1,0:T(8,128)(2,1)}), bf16[16,32,512]{2,1,0:T(8,128)(2,1)S(1)}, u32[]{:S(2)}, u32[]{:S(2)}) async-start(bf16[16,32,512]{2,1,0:T(8,128)(2,1)} %broadcast_in_dim.3), calls=%async_computation.2 | async-start | bytes 1048576 | tf_op jit(solution)/shard_map/all_to_all | solution.py:281
  118.5 5.7 %copy-start.3 = (bf16[512,16000]{1,0:T(8,128)(2,1)S(1)}, bf16[512,16000]{1,0:T(8,128)(2,1)}, u32[]{:S(2)}) copy-start(bf16[512,16000]{1,0:T(8,128)(2,1)} %copy-done) | copy-start | bytes 49152004
  133.6 18.1 %all-to-all-start.4 = ((bf16[16,32,384]{2,1,0:T(8,128)(2,1)}), bf16[16,32,384]{2,1,0:T(8,128)(2,1)S(1)}, u32[]{:S(2)}, u32[]{:S(2)}) async-start(bf16[16,32,384]{2,1,0:T(8,128)(2,1)} %get-tuple-element.27), calls=%async_computation.4 | async-start | bytes 786432 | tf_op jit(solution)/shard_map/all_to_all | solution.py:281

commit v3 on v2

v3 whole, which is shorter than its diff:
```python
import jax
import jax.numpy as jnp
from jax import lax
from jax.experimental import pallas as pl
from jax.experimental.pallas import tpu as pltpu
from jax.sharding import PartitionSpec as P

center = 6.0
half_width = 4.0
LO = 512
GLO = 128
STEP = 8
UNROLL = 4


def sweep(steps, body):
    def group(number, carry):
        for place in range(UNROLL):
            body(number * UNROLL + place)
        return carry

    lax.fori_loop(0, steps // UNROLL, group, 0)


def flags(row, width):
    parts = []
    level = lax.broadcasted_iota(jnp.int32, (min(width, 256), 128), 0)
    level = level.astype(jnp.float32).astype(jnp.bfloat16)
    one = jnp.ones(level.shape, jnp.bfloat16)
    zero = jnp.zeros(level.shape, jnp.bfloat16)
    for base in range(0, width, level.shape[0]):
        local = row - base
        local = jnp.where((local >= 0) & (local < level.shape[0]), local, -1)
        local = local.astype(jnp.float32).astype(jnp.bfloat16)
        parts.append(jnp.where(level == jnp.broadcast_to(local, level.shape), one, zero))
    return parts[0] if len(parts) == 1 else jnp.concatenate(parts, axis=0)


def low_part(row, width):
    return jnp.bitwise_and(row, width - 1)


def high_part(row, width):
    return jnp.right_shift(row, width.bit_length() - 1)


def choose(product, highs, count):
    groups = product.shape[0] // count
    picked = []
    for k, high in enumerate(highs):
        total = jnp.zeros((count, 128), jnp.float32)
        for group in range(groups):
            part = product[group * count : (group + 1) * count, k * 128 : (k + 1) * 128]
            total = jnp.where(high == group, part, total)
        picked.append(total)
    return picked


def row_list(block):
    return [block[k : k + 1, :] for k in range(block.shape[0])]


def stack_groups(field_ref, table_ref, count):
    for group in range(field_ref.shape[1] // LO):
        table_ref[group * count : (group + 1) * count, :] = field_ref[
            :, group * LO : (group + 1) * LO
        ]


class Copies:
    def __init__(self, sems):
        self.sems = sems
        self.used = 0

    def start(self, source, target):
        copy = pltpu.make_async_copy(source, target, self.sems.at[self.used])
        copy.start()
        self.used += 1
        return copy


def marks_of(block, width):
    return jnp.concatenate([flags(low_part(row, width), width) for row in row_list(block)], axis=1)


def read_map(copies, map_hbm, map_ref):
    npe = map_hbm.shape[0]
    return copies.start(map_hbm, map_ref.at[:npe])


def fill_map(map_ref, npe):
    rest = map_ref.shape[0] - npe
    map_ref[npe:, :] = jnp.full((rest, map_ref.shape[1]), -1, jnp.int32)


def block_of(ref, number):
    return ref[pl.ds(pl.multiple_of(number * STEP, STEP), STEP), :]


def pack_sends(table_ref, send_ref, nbr_ref, out_ref, count):
    out_ref[...] = jnp.zeros(out_ref.shape, out_ref.dtype)
    rows = [
        jnp.concatenate([send_ref[k], send_ref[k + 1]], axis=1)
        for k in range(0, send_ref.shape[0], 2)
    ]
    marks = jnp.concatenate([flags(low_part(row, LO), LO) for row in rows], axis=1)
    product = jnp.dot(table_ref[...], marks, preferred_element_type=jnp.float32)
    picked = choose(product, [high_part(row, LO) for row in rows], count)
    half = count // 2
    for k, part in enumerate(picked):
        for side in range(2):
            block = part[:, side * 64 : (side + 1) * 64]
            tile = jnp.concatenate([block[:half], block[half:]], axis=1)
            out_ref[nbr_ref[0, 2 * k + side]] = tile.astype(jnp.bfloat16)


def pack_kernel(
    nbr_hbm, field_hbm, send_hbm, out_hbm, field_ref, send_ref, table_ref, out_ref, nbr_ref, sems
):
    copies = Copies(sems)
    nbr_copy = copies.start(nbr_hbm, nbr_ref)
    field_copy = copies.start(field_hbm, field_ref)
    send_copy = copies.start(send_hbm, send_ref)
    count = field_ref.shape[0]
    field_copy.wait()
    stack_groups(field_ref, table_ref, count)
    send_copy.wait()
    nbr_copy.wait()
    pack_sends(table_ref, send_ref, nbr_ref, out_ref, count)
    copies.start(out_ref, out_hbm).wait()


def gather_chunk(table, block, marks, own_ref, number, count):
    product = jnp.dot(table, marks, preferred_element_type=jnp.float32)
    highs = [high_part(row, LO) for row in row_list(block)]
    for k, part in enumerate(choose(product, highs, count)):
        own_ref[number * STEP + k] = part.astype(jnp.bfloat16)


def gather_kernel(field_hbm, map_hbm, rows_hbm, own_hbm, copies_hbm, field_ref, map_ref, rows_ref, own_ref, table_ref, sems):
    copies = Copies(sems)
    field_copy = copies.start(field_hbm, field_ref)
    map_copy = read_map(copies, map_hbm, map_ref)
    rows_copy = copies.start(rows_hbm, rows_ref)
    count = field_ref.shape[0]
    field_copy.wait()
    stack_groups(field_ref, table_ref, count)
    rows_copy.wait()
    pending = [copies.start(rows_ref, copies_hbm.at[k]) for k in range(copies_hbm.shape[0])]
    map_copy.wait()
    fill_map(map_ref, map_hbm.shape[0])

    def body(number):
        block = block_of(map_ref, number)
        gather_chunk(table_ref[...], block, marks_of(block, LO), own_ref, number, count)

    sweep(map_ref.shape[0] // STEP, body)
    copies.start(own_ref, own_hbm).wait()
    for copy in pending:
        copy.wait()


def contract(
    copies, nbr_hbm, own_hbm, recv_hbm, map_hbm, kernel_hbm, scale_hbm,
    own_ref, recv_ref, map_ref, kernel_ref, scale_ref,
    ghost_ref, square_ref, nodes_ref, product_ref, nbr_ref, nodes, later,
):
    count = own_ref.shape[1]
    npe = kernel_hbm.shape[0]
    half = count // 2
    nbr_copy = copies.start(nbr_hbm, nbr_ref)
    recv_copy = copies.start(recv_hbm, recv_ref)
    map_copy = read_map(copies, map_hbm, map_ref)
    own_copy = copies.start(own_hbm, own_ref)
    kernel_copy = copies.start(kernel_hbm, kernel_ref)
    scale_copy = copies.start(scale_hbm, scale_ref)
    rest = later()
    square_ref[...] = jnp.zeros(square_ref.shape, square_ref.dtype)
    nbr_copy.wait()
    neighbours = [nbr_ref[0, position] for position in range(nbr_ref.shape[1])]
    recv_copy.wait()
    for k in range(ghost_ref.shape[0] // count):
        left = recv_ref[neighbours[2 * k]]
        right = recv_ref[neighbours[2 * k + 1]]
        ghost_ref[k * count : k * count + half, :] = jnp.concatenate(
            [left[:, :64], right[:, :64]], axis=1
        )
        ghost_ref[k * count + half : (k + 1) * count, :] = jnp.concatenate(
            [left[:, 64:], right[:, 64:]], axis=1
        )
    map_copy.wait()
    fill_map(map_ref, map_hbm.shape[0])
    own_copy.wait()

    def body(number):
        slot = block_of(map_ref, number) - nodes
        owner = jnp.right_shift(slot, 6)
        place = jnp.full(slot.shape, -1, jnp.int32)
        for position, neighbour in enumerate(neighbours):
            place = jnp.where(owner == neighbour, position, place)
        compact = jnp.where(place >= 0, place * 64 + jnp.bitwise_and(slot, 63), -1)
        product = jnp.dot(
            ghost_ref[...], marks_of(compact, GLO), preferred_element_type=jnp.float32
        )
        highs = [high_part(row, GLO) for row in row_list(compact)]
        for k, part in enumerate(choose(product, highs, count)):
            base = number * STEP + k
            nodes_ref[base] = part + own_ref[base].astype(jnp.float32)

    sweep(map_ref.shape[0] // STEP, body)
    kernel_copy.wait()
    square_ref[:npe, :npe] = kernel_ref[...]
    scale_copy.wait()
    scale = scale_ref[...]
    for state in range(0, count, 2):
        columns = jnp.concatenate(
            [nodes_ref[:, state, :], nodes_ref[:, state + 1, :]], axis=1
        ).astype(jnp.bfloat16)
        product = jnp.dot(square_ref[...], columns, preferred_element_type=jnp.float32)
        product_ref[:, state, :] = product[:, :128] * scale
        product_ref[:, state + 1, :] = product[:, 128:] * scale
    return rest


def scatter(map_ref, product_ref, total_ref, count):
    groups = total_ref.shape[0] // count
    zero = jnp.zeros((count, 128), jnp.bfloat16)
    total_ref[...] = jnp.zeros(total_ref.shape, jnp.float32)

    def body(number):
        block = block_of(map_ref, number)
        parts = []
        for k, row in enumerate(row_list(block)):
            high = high_part(row, LO).astype(jnp.float32).astype(jnp.bfloat16)
            high = jnp.broadcast_to(high, zero.shape)
            value = product_ref[number * STEP + k].astype(jnp.bfloat16)
            parts.append(
                jnp.concatenate(
                    [
                        jnp.where(high == jnp.full(zero.shape, group, jnp.bfloat16), value, zero)
                        for group in range(groups)
                    ],
                    axis=0,
                )
            )
        total_ref[...] += lax.dot_general(
            jnp.concatenate(parts, axis=1), marks_of(block, LO), (((1,), (1,)), ((), ())),
            preferred_element_type=jnp.float32,
        )

    sweep(map_ref.shape[0] // STEP, body)


def first_kernel(
    nbr_hbm, own_hbm, recv_hbm, map_hbm, kernel_hbm, scale_hbm, field_hbm, pot_hbm, send_hbm,
    next_hbm, out_hbm,
    own_ref, recv_ref, map_ref, kernel_ref, scale_ref,
    ghost_ref, square_ref, nodes_ref, product_ref,
    field_ref, pot_ref, send_ref, next_ref, table_ref, total_ref, out_ref,
    nbr_ref, sems,
):
    copies = Copies(sems)
    count, nodes = field_ref.shape

    def later():
        return [
            copies.start(field_hbm, field_ref),
            copies.start(pot_hbm, pot_ref),
            copies.start(send_hbm, send_ref),
        ]

    others = contract(
        copies, nbr_hbm, own_hbm, recv_hbm, map_hbm, kernel_hbm, scale_hbm,
        own_ref, recv_ref, map_ref, kernel_ref, scale_ref,
        ghost_ref, square_ref, nodes_ref, product_ref, nbr_ref, nodes, later,
    )
    scatter(map_ref, product_ref, total_ref, count)
    for copy in others:
        copy.wait()
    for group in range(field_ref.shape[1] // LO):
        lanes = slice(group * LO, (group + 1) * LO)
        rows = slice(group * count, (group + 1) * count)
        start = field_ref[:, lanes].astype(jnp.float32)
        image = total_ref[rows, :] + pot_ref[:, lanes] * start
        field = ((image - center * start) / half_width).astype(jnp.bfloat16)
        next_ref[:, lanes] = field
        table_ref[rows, :] = field
    next_copy = copies.start(next_ref, next_hbm)
    pack_sends(table_ref, send_ref, nbr_ref, out_ref, count)
    copies.start(out_ref, out_hbm).wait()
    next_copy.wait()


def energy_kernel(
    nbr_hbm, own_hbm, recv_hbm, map_hbm, kernel_hbm, scale_hbm, field_hbm, pot_hbm,
    cells_hbm, energy_ref,
    own_ref, recv_ref, map_ref, kernel_ref, scale_ref,
    ghost_ref, square_ref, nodes_ref, product_ref, field_ref, pot_ref, cells_ref, nbr_ref, sems,
):
    copies = Copies(sems)
    count, nodes = field_ref.shape

    def later():
        return [copies.start(field_hbm, field_ref), copies.start(pot_hbm, pot_ref)]

    others = contract(
        copies, nbr_hbm, own_hbm, recv_hbm, map_hbm, kernel_hbm, scale_hbm,
        own_ref, recv_ref, map_ref, kernel_ref, scale_ref,
        ghost_ref, square_ref, nodes_ref, product_ref, nbr_ref, nodes, later,
    )
    total = jnp.zeros((count, 128), jnp.float32)
    for base in range(own_ref.shape[0]):
        value = product_ref[base]
        cells_ref[base] = value.astype(jnp.bfloat16)
        total = total + value * own_ref[base].astype(jnp.float32)
    cells_copy = copies.start(cells_ref, cells_hbm)
    for copy in others:
        copy.wait()
    for base in range(0, nodes, 128):
        one = field_ref[:, base : base + 128].astype(jnp.float32)
        total = total + pot_ref[:, base : base + 128] * one * one
    sums = jnp.broadcast_to(jnp.sum(total, axis=1, keepdims=True), total.shape)
    state = lax.broadcasted_iota(jnp.int32, total.shape, 0)
    lane = lax.broadcasted_iota(jnp.int32, total.shape, 1)
    line = jnp.sum(jnp.where(state == lane, sums, 0.0), axis=0, keepdims=True)
    energy_ref[...] = jnp.broadcast_to(line[None], energy_ref.shape)
    cells_copy.wait()


def second_kernel(
    field_hbm, cells_hbm, map_hbm, pot_hbm, start_hbm, next_hbm, out_hbm,
    field_ref, cells_ref, map_ref, pot_ref, start_ref, next_ref, total_ref, sems,
):
    copies = Copies(sems)
    count = field_ref.shape[0]
    map_copy = read_map(copies, map_hbm, map_ref)
    cell_copy = copies.start(cells_hbm, cells_ref)
    others = [
        copies.start(field_hbm, field_ref),
        copies.start(pot_hbm, pot_ref),
        copies.start(start_hbm, start_ref),
    ]
    map_copy.wait()
    fill_map(map_ref, map_hbm.shape[0])
    cell_copy.wait()
    scatter(map_ref, cells_ref, total_ref, count)
    for copy in others:
        copy.wait()
    for group in range(field_ref.shape[1] // LO):
        lanes = slice(group * LO, (group + 1) * LO)
        rows = slice(group * count, (group + 1) * count)
        one = field_ref[:, lanes].astype(jnp.float32)
        start = start_ref[:, lanes].astype(jnp.float32)
        image = total_ref[rows, :] + pot_ref[:, lanes] * one
        next_ref[:, lanes] = (
            2.0 * (image - center * one) / half_width - start
        ).astype(jnp.bfloat16)
    width = out_hbm.shape[2]
    pending = [copies.start(next_ref, next_hbm)]
    for band in range(out_hbm.shape[0]):
        pending.append(
            copies.start(next_ref.at[:, band * width : (band + 1) * width], out_hbm.at[band])
        )
    for copy in pending:
        copy.wait()


def rotate_kernel(owner_hbm, rows_hbm, states_hbm, out_hbm, rows_ref, states_ref, out_ref, owner_ref, sems):
    copies = Copies(sems)
    copies.start(owner_hbm, owner_ref).wait()
    pending = []
    count = rows_hbm.shape[1]
    for k in range(owner_ref.shape[0]):
        place = pl.ds(k * count, count)
        pending.append(copies.start(rows_hbm.at[owner_ref[k]], rows_ref.at[place]))
        pending.append(copies.start(states_hbm.at[owner_ref[k]], states_ref.at[place]))
    for copy in pending:
        copy.wait()
    out_ref[...] = lax.dot_general(
        rows_ref[...], states_ref[...], (((0,), (0,)), ((), ())),
        preferred_element_type=jnp.float32,
    ).astype(jnp.bfloat16)
    copies.start(out_ref, out_hbm).wait()


vmem = pl.BlockSpec(memory_space=pltpu.VMEM)
hbm = pl.BlockSpec(memory_space=pltpu.HBM)
anywhere = pl.BlockSpec(memory_space=pl.ANY)
half = jnp.bfloat16
full = jnp.float32
whole = jnp.int32


def call(kernel, name, outs, scratch, scalars, sems, *operands, free=-1):
    held = [
        value if k == free else pltpu.with_memory_space_constraint(value, pltpu.HBM)
        for k, value in enumerate(operands)
    ]
    return pl.pallas_call(
        kernel,
        out_shape=tuple(
            jax.ShapeDtypeStruct(dims, kind) if place is vmem else pltpu.HBM(dims, kind)
            for dims, kind, place in outs
        ),
        in_specs=[anywhere if k == free else hbm for k in range(len(operands))],
        out_specs=tuple(place for _, _, place in outs),
        scratch_shapes=[pltpu.VMEM(dims, kind) for dims, kind in scratch]
        + [pltpu.SMEM(dims, jnp.int32) for dims in scalars]
        + [pltpu.SemaphoreType.DMA((sems,))],
        compiler_params=pltpu.CompilerParams(vmem_limit_bytes=48 << 20),
        name=name,
    )(*held)


def swap(value, axis):
    return lax.all_to_all(value, axis, split_axis=0, concat_axis=0, tiled=True)


def per_device(
    filter_block,
    local_pot,
    cell_scale,
    cell_kernel,
    cell_map,
    neighbour_ids,
    send_nodes,
    rotation_rows,
    panel_owner,
):
    count, nodes = filter_block.shape
    npe, cells = cell_map.shape
    mesh_size = lax.axis_size("mesh")
    band_size = lax.axis_size("band")
    width = nodes // band_size
    sends = send_nodes.transpose(1, 0, 2)
    pot = local_pot.reshape(1, -1)
    scale = cell_scale.reshape(1, -1)
    steps = -(-npe // (STEP * UNROLL)) * UNROLL
    padded = steps * STEP

    field_type = ((count, nodes), half)
    map_type = ((padded, cells), whole)
    send_type = (sends.shape, whole)
    pot_type = (pot.shape, full)
    table = ((nodes // LO * count, LO), half)
    total = ((nodes // LO * count, LO), full)
    outbox = ((mesh_size, count // 2, 128), half)
    columns = ((padded, count, cells), half)
    rows_type = (rotation_rows.shape, half)
    nbr_type = neighbour_ids.shape
    inner = [
        columns, outbox, map_type, (cell_kernel.shape, half), (scale.shape, full),
        ((send_nodes.size // GLO * count, GLO), half),
        ((padded, padded), half),
        ((padded, count, cells), full),
        ((padded, count, cells), full),
    ]

    (outgoing,) = call(
        pack_kernel, "pack", [outbox + (hbm,)], [field_type, send_type, table, outbox],
        [nbr_type], 4, neighbour_ids, filter_block, sends,
    )
    incoming = swap(outgoing, "mesh")
    copies_type = ((band_size,) + rotation_rows.shape, half)

    def gather(field):
        return call(
            gather_kernel, "gather", [columns + (hbm,), copies_type + (hbm,)],
            [field_type, map_type, rows_type, columns, table], [], 4 + band_size,
            field, cell_map, rotation_rows,
        )

    own, row_copies = gather(filter_block)
    field_one, outgoing = call(
        first_kernel, "first", [field_type + (hbm,), outbox + (hbm,)],
        inner + [field_type, pot_type, send_type, field_type, table, total, outbox],
        [nbr_type], 11, neighbour_ids, own, incoming, cell_map, cell_kernel, scale,
        filter_block, pot, sends, free=2,
    )
    all_rows = swap(row_copies, "band")
    outgoing, all_rows = lax.optimization_barrier((outgoing, all_rows))
    incoming = swap(outgoing, "mesh")
    own, _ = gather(field_one)
    products, energy = call(
        energy_kernel, "energy", [columns + (hbm,), ((mesh_size, 1, 128), full, vmem)],
        inner + [field_type, pot_type, columns], [nbr_type], 9,
        neighbour_ids, own, incoming, cell_map, cell_kernel, scale, field_one, pot, free=2,
    )
    energies = swap(energy, "mesh")
    filtered, parts = call(
        second_kernel, "second",
        [field_type + (hbm,), ((band_size, count, width), half, hbm)],
        [field_type, columns, map_type, pot_type, field_type, field_type, total],
        [], 6 + band_size, field_one, products, cell_map, pot, filter_block,
    )
    parts, energies = lax.optimization_barrier((parts, energies))
    states = swap(parts, "band")
    state_energy = jnp.sum(energies[:, 0, :count], axis=0) / (nodes * mesh_size)
    rotated_type = ((rotation_rows.shape[1], width), half)
    (rotated,) = call(
        rotate_kernel, "rotate", [rotated_type + (hbm,)],
        [
            ((panel_owner.size * count, rotation_rows.shape[1]), half),
            ((panel_owner.size * count, width), half),
            rotated_type,
        ],
        [panel_owner.shape], 2 + 2 * panel_owner.size, panel_owner, all_rows, states, free=2,
    )
    return (filtered, rotated, state_energy)


def solution(mesh):
    placed = (
        P("band", "mesh"),
        P("mesh"),
        P("mesh"),
        P(),
        P(None, "mesh"),
        P("mesh", None),
        P("mesh", None, None),
        P("band", None),
        P(),
    )
    return jax.shard_map(
        per_device,
        mesh=mesh,
        in_specs=placed,
        out_specs=(P("band", "mesh"), P(None, ("mesh", "band")), P("band")),
        check_vma=False,
    )
```

time: 154 us -> 122 us (0.79)
  the two profiles are of different devices: /device:TPU:10 before, /device:TPU:14 now
where the time goes in v3:
time: 122 us; the launch traced here: 121 us
  Pallas kernels  57.7 us (47%)
  starting transfers between devices  49.4 us (40%)
  waiting for transfers between devices  12.7 us (10%)
    pallas_call x7, Pallas kernels, call(): pl.pallas_call(kernel, out_shape=tuple((jax.ShapeDtypeStruct(dims, kind)...  57.7 us
    all_to_all x5, starting transfers between devices, swap(): return lax.all_to_all(value, axis, split_axis=0, concat_axis=0, tiled=True)  49.4 us
    all_to_all x5, waiting for transfers between devices, swap(): return lax.all_to_all(value, axis, split_axis=0, concat_axis=0, tiled=True)  12.7 us
  transfers between devices with their start and end apart: 5, of which 2 were waited for; matrix products, arithmetic and copies ran while one was open for 0% of the time, Pallas kernels for 36%

profile of v3, /device:TPU:14, one launch (start us, length us, event | category | flops | bytes accessed | tf_op | source)
XLA Modules:
  0.0 121.3 jit_solution(7645617133283081122)
XLA Ops:
  0.6 2.5 %pack.1 = bf16[32,16,128]{2,1,0:T(8,128)(2,1)} custom-call(s32[1,14]{1,0:T(1,128)} %nbr_hbm.5, bf16[32,6144]{1,0:T(8,128)(2,1)} %start_hbm.1, s32[14,1,64]{2,1,0:T(1,128)} %bitcast.6), custom_call_target="tpu_custom_call" | custom-call | tf_op jit(solution)/shard_map/pack/pallas_call | solution.py:399
  3.1 13.5 %all-to-all-start = ((bf16[32,16,128]{2,1,0:T(8,128)(2,1)}), bf16[32,16,128]{2,1,0:T(8,128)(2,1)S(1)}, u32[]{:S(2)}, u32[]{:S(2)}) async-start(bf16[32,16,128]{2,1,0:T(8,128)(2,1)} %pack.1), calls=%async_computation | async-start | bytes 262144 | tf_op jit(solution)/shard_map/all_to_all | solution.py:416
  16.6 9.4 %gather.2 = (bf16[128,32,128]{2,1,0:T(8,128)(2,1)}, bf16[16,32,512]{2,1,0:T(8,128)(2,1)}) custom-call(bf16[32,6144]{1,0:T(8,128)(2,1)} %start_hbm.1, s32[125,128]{1,0:T(8,128)} %map_hbm.9, bf16[32,512]{1,0:T(8,128)(2,1)} %rows_hbm.3), custom_call_target="tpu_custom_call" | custom-call | tf_op jit(solution)/shard_map/gather/pallas_call | solution.py:399
  26.0 0.0 all-to-all-done.recv_hbm
  26.0 8.5 %all-to-all-start.1 = ((bf16[16,32,512]{2,1,0:T(8,128)(2,1)}), bf16[16,32,512]{2,1,0:T(8,128)(2,1)S(1)}, u32[]{:S(2)}, u32[]{:S(2)}) async-start(bf16[16,32,512]{2,1,0:T(8,128)(2,1)} %get-tuple-element.20), calls=%async_computation.1 | async-start | bytes 1048576 | tf_op jit(solution)/shard_map/all_to_all | solution.py:416
  34.5 15.3 %first.1 = (bf16[32,6144]{1,0:T(8,128)(2,1)}, bf16[32,16,128]{2,1,0:T(8,128)(2,1)}) custom-call(s32[1,14]{1,0:T(1,128)} %nbr_hbm.5, bf16[128,32,128]{2,1,0:T(8,128)(2,1)} %get-tuple-element.16.own_hbm, bf16[32,16,128]{2,1,0:T(8,128)(2,1)S(1)} %all-to-all-done.recv_hbm, s32[125,128]{1,0:T(8,128)} %map_hbm.9, bf16[125,125]{1,0:T(8,128)(2,1)} %kernel_hbm.3, ...), custom_call_target="tpu_custom_call" | custom-call | tf_op jit(solution)/shard_map/first/pallas_call | solution.py:399
  49.8 0.3 all-to-all-done.1.rows_hbm
  50.1 0.0 copy-start
  50.1 9.8 %all-to-all-start.2 = ((bf16[32,16,128]{2,1,0:T(8,128)(2,1)}), bf16[32,16,128]{2,1,0:T(8,128)(2,1)S(1)}, u32[]{:S(2)}, u32[]{:S(2)}) async-start(bf16[32,16,128]{2,1,0:T(8,128)(2,1)} %get-tuple-element.21), calls=%async_computation.2 | async-start | bytes 262144 | tf_op jit(solution)/shard_map/all_to_all | solution.py:416
  60.0 9.4 %gather.3 = (bf16[128,32,128]{2,1,0:T(8,128)(2,1)}, bf16[16,32,512]{2,1,0:T(8,128)(2,1)}) custom-call(bf16[32,6144]{1,0:T(8,128)(2,1)} %get-tuple-element.17.field_hbm, s32[125,128]{1,0:T(8,128)} %map_hbm.9, bf16[32,512]{1,0:T(8,128)(2,1)} %rows_hbm.3), custom_call_target="tpu_custom_call" | custom-call | tf_op jit(solution)/shard_map/gather/pallas_call | solution.py:399
  69.4 0.0 all-to-all-done.2.recv_hbm
  69.4 8.5 %energy.1 = (bf16[128,32,128]{2,1,0:T(8,128)(2,1)}, f32[32,1,128]{2,1,0:T(1,128)}) custom-call(s32[1,14]{1,0:T(1,128)} %nbr_hbm.5, bf16[128,32,128]{2,1,0:T(8,128)(2,1)} %get-tuple-element.18.own_hbm, bf16[32,16,128]{2,1,0:T(8,128)(2,1)S(1)} %all-to-all-done.2.recv_hbm, s32[125,128]{1,0:T(8,128)} %map_hbm.9, bf16[125,125]{1,0:T(8,128)(2,1)} %kernel_hbm.3, ...), custom_call_target="tpu_custom_call" | custom-call | tf_op jit(solution)/shard_map/energy/pallas_call | solution.py:399
  78.0 0.0 copy-done
  78.0 9.8 %all-to-all-start.3 = ((f32[32,1,128]{2,1,0:T(1,128)}), f32[32,1,128]{2,1,0:T(1,128)S(1)}, u32[]{:S(2)}, u32[]{:S(2)}) async-start(f32[32,1,128]{2,1,0:T(1,128)} %get-tuple-element.26), calls=%async_computation.3 | async-start | bytes 32768 | tf_op jit(solution)/shard_map/all_to_all | solution.py:416
  87.8 9.9 %second.1 = (bf16[32,6144]{1,0:T(8,128)(2,1)}, bf16[16,32,384]{2,1,0:T(8,128)(2,1)}) custom-call(bf16[32,6144]{1,0:T(8,128)(2,1)} %get-tuple-element.17.field_hbm, bf16[128,32,128]{2,1,0:T(8,128)(2,1)} %get-tuple-element.22.cells_hbm, s32[125,128]{1,0:T(8,128)} %map_hbm.9, f32[1,6144]{1,0:T(1,128)} %bitcast.5, bf16[32,6144]{1,0:T(8,128)(2,1)} %start_hbm.1), custom_call_target="tpu_custom_call" | custom-call | tf_op jit(solution)/shard_map/second/pallas_call | solution.py:399
  97.8 0.0 all-to-all-done.3
  97.8 7.9 %all-to-all-start.4 = ((bf16[16,32,384]{2,1,0:T(8,128)(2,1)}), bf16[16,32,384]{2,1,0:T(8,128)(2,1)S(1)}, u32[]{:S(2)}, u32[]{:S(2)}) async-start(bf16[16,32,384]{2,1,0:T(8,128)(2,1)} %get-tuple-element.27), calls=%async_computation.4 | async-start | bytes 786432 | tf_op jit(solution)/shard_map/all_to_all | solution.py:416
  105.6 0.1 slice_reduce_fusion
  105.7 0.5 broadcast_multiply_fusion
  106.2 12.4 %all-to-all-done.4.states_hbm = bf16[16,32,384]{2,1,0:T(8,128)(2,1)S(1)} async-done(((bf16[16,32,384]{2,1,0:T(8,128)(2,1)}), bf16[16,32,384]{2,1,0:T(8,128)(2,1)S(1)}, u32[]{:S(2)}, u32[]{:S(2)}) %all-to-all-start.4) | async-done | bytes 393248 | tf_op jit(solution)/shard_map/all_to_all | solution.py:416
  118.6 2.5 %rotate.1 = bf16[512,384]{1,0:T(8,128)(2,1)} custom-call(s32[2]{0:T(128)} %owner_hbm.1, bf16[16,32,512]{2,1,0:T(8,128)(2,1)} %copy-done, bf16[16,32,384]{2,1,0:T(8,128)(2,1)S(1)} %all-to-all-done.4.states_hbm), custom_call_target="tpu_custom_call" | custom-call | tf_op jit(solution)/shard_map/rotate/pallas_call | solution.py:399
Async XLA Ops:
  3.1 22.9 %all-to-all-start = ((bf16[32,16,128]{2,1,0:T(8,128)(2,1)}), bf16[32,16,128]{2,1,0:T(8,128)(2,1)S(1)}, u32[]{:S(2)}, u32[]{:S(2)}) async-start(bf16[32,16,128]{2,1,0:T(8,128)(2,1)} %pack.1), calls=%async_computation | async-start | bytes 262144 | tf_op jit(solution)/shard_map/all_to_all | solution.py:416
  26.0 24.1 %all-to-all-start.1 = ((bf16[16,32,512]{2,1,0:T(8,128)(2,1)}), bf16[16,32,512]{2,1,0:T(8,128)(2,1)S(1)}, u32[]{:S(2)}, u32[]{:S(2)}) async-start(bf16[16,32,512]{2,1,0:T(8,128)(2,1)} %get-tuple-element.20), calls=%async_computation.1 | async-start | bytes 1048576 | tf_op jit(solution)/shard_map/all_to_all | solution.py:416
  50.1 27.8 %copy-start = (bf16[16,32,512]{2,1,0:T(8,128)(2,1)}, bf16[16,32,512]{2,1,0:T(8,128)(2,1)S(1)}, u32[]{:S(2)}) copy-start(bf16[16,32,512]{2,1,0:T(8,128)(2,1)S(1)} %all-to-all-done.1.rows_hbm) | copy-start | bytes 1572868
  50.1 19.3 %all-to-all-start.2 = ((bf16[32,16,128]{2,1,0:T(8,128)(2,1)}), bf16[32,16,128]{2,1,0:T(8,128)(2,1)S(1)}, u32[]{:S(2)}, u32[]{:S(2)}) async-start(bf16[32,16,128]{2,1,0:T(8,128)(2,1)} %get-tuple-element.21), calls=%async_computation.2 | async-start | bytes 262144 | tf_op jit(solution)/shard_map/all_to_all | solution.py:416
  78.0 19.8 %all-to-all-start.3 = ((f32[32,1,128]{2,1,0:T(1,128)}), f32[32,1,128]{2,1,0:T(1,128)S(1)}, u32[]{:S(2)}, u32[]{:S(2)}) async-start(f32[32,1,128]{2,1,0:T(1,128)} %get-tuple-element.26), calls=%async_computation.3 | async-start | bytes 32768 | tf_op jit(solution)/shard_map/all_to_all | solution.py:416
  97.8 20.9 %all-to-all-start.4 = ((bf16[16,32,384]{2,1,0:T(8,128)(2,1)}), bf16[16,32,384]{2,1,0:T(8,128)(2,1)S(1)}, u32[]{:S(2)}, u32[]{:S(2)}) async-start(bf16[16,32,384]{2,1,0:T(8,128)(2,1)} %get-tuple-element.27), calls=%async_computation.4 | async-start | bytes 786432 | tf_op jit(solution)/shard_map/all_to_all | solution.py:416

commit v4 on v3

--- a/solution.py
+++ b/solution.py
@@ -10,7 +10,7 @@
 LO = 512
 GLO = 128
 STEP = 8
-UNROLL = 4
+UNROLL = 8
 
 
 def sweep(steps, body):
@@ -115,19 +115,33 @@
 
 
 def pack_kernel(
-    nbr_hbm, field_hbm, send_hbm, out_hbm, field_ref, send_ref, table_ref, out_ref, nbr_ref, sems
+    nbr_hbm, owner_hbm, field_hbm, send_hbm, rows_hbm, out_hbm, panel_hbm,
+    field_ref, send_ref, table_ref, rows_ref, panel_ref, out_ref, nbr_ref, owner_ref, sems,
 ):
     copies = Copies(sems)
-    nbr_copy = copies.start(nbr_hbm, nbr_ref)
     field_copy = copies.start(field_hbm, field_ref)
     send_copy = copies.start(send_hbm, send_ref)
+    owner_copy = copies.start(owner_hbm, owner_ref)
+    rows_copy = copies.start(rows_hbm, rows_ref)
+    nbr_copy = copies.start(nbr_hbm, nbr_ref)
     count = field_ref.shape[0]
+    mine = lax.axis_index("band")
+    owner_copy.wait()
+    rows_copy.wait()
+    rows = rows_ref[...].astype(jnp.float32)
+    for k in range(owner_ref.shape[0]):
+        panel_ref[k * count : (k + 1) * count, :] = jnp.where(
+            owner_ref[k] == mine, rows, jnp.zeros_like(rows)
+        ).astype(jnp.bfloat16)
+    pending = [copies.start(panel_ref, panel_hbm.at[k]) for k in range(panel_hbm.shape[0])]
     field_copy.wait()
     stack_groups(field_ref, table_ref, count)
     send_copy.wait()
     nbr_copy.wait()
     pack_sends(table_ref, send_ref, nbr_ref, out_ref, count)
-    copies.start(out_ref, out_hbm).wait()
+    pending.append(copies.start(out_ref, out_hbm))
+    for copy in pending:
+        copy.wait()
 
 
 def gather_chunk(table, block, marks, own_ref, number, count):
@@ -137,16 +151,13 @@
         own_ref[number * STEP + k] = part.astype(jnp.bfloat16)
 
 
-def gather_kernel(field_hbm, map_hbm, rows_hbm, own_hbm, copies_hbm, field_ref, map_ref, rows_ref, own_ref, table_ref, sems):
+def gather_kernel(field_hbm, map_hbm, own_hbm, field_ref, map_ref, own_ref, table_ref, sems):
     copies = Copies(sems)
     field_copy = copies.start(field_hbm, field_ref)
     map_copy = read_map(copies, map_hbm, map_ref)
-    rows_copy = copies.start(rows_hbm, rows_ref)
     count = field_ref.shape[0]
     field_copy.wait()
     stack_groups(field_ref, table_ref, count)
-    rows_copy.wait()
-    pending = [copies.start(rows_ref, copies_hbm.at[k]) for k in range(copies_hbm.shape[0])]
     map_copy.wait()
     fill_map(map_ref, map_hbm.shape[0])
 
@@ -156,8 +167,6 @@
 
     sweep(map_ref.shape[0] // STEP, body)
     copies.start(own_ref, own_hbm).wait()
-    for copy in pending:
-        copy.wait()
 
 
 def contract(
@@ -365,15 +374,19 @@
         copy.wait()
 
 
-def rotate_kernel(owner_hbm, rows_hbm, states_hbm, out_hbm, rows_ref, states_ref, out_ref, owner_ref, sems):
+def rotate_kernel(
+    owner_hbm, rows_hbm, states_hbm, out_hbm, rows_ref, states_ref, out_ref, owner_ref, sems
+):
     copies = Copies(sems)
-    copies.start(owner_hbm, owner_ref).wait()
-    pending = []
-    count = rows_hbm.shape[1]
-    for k in range(owner_ref.shape[0]):
-        place = pl.ds(k * count, count)
-        pending.append(copies.start(rows_hbm.at[owner_ref[k]], rows_ref.at[place]))
-        pending.append(copies.start(states_hbm.at[owner_ref[k]], states_ref.at[place]))
+    owner_copy = copies.start(owner_hbm, owner_ref)
+    rows_copy = copies.start(rows_hbm, rows_ref)
+    owner_copy.wait()
+    count = states_hbm.shape[1]
+    pending = [
+        copies.start(states_hbm.at[owner_ref[k]], states_ref.at[pl.ds(k * count, count)])
+        for k in range(owner_ref.shape[0])
+    ]
+    rows_copy.wait()
     for copy in pending:
         copy.wait()
     out_ref[...] = lax.dot_general(
@@ -456,31 +469,30 @@
         ((padded, count, cells), full),
     ]
 
-    (outgoing,) = call(
-        pack_kernel, "pack", [outbox + (hbm,)], [field_type, send_type, table, outbox],
-        [nbr_type], 4, neighbour_ids, filter_block, sends,
-    )
+    panel_type = ((panel_owner.size * count, rotation_rows.shape[1]), half)
+    outgoing, panels = call(
+        pack_kernel, "pack", [outbox + (hbm,), ((band_size,) + panel_type[0], half, hbm)],
+        [field_type, send_type, table, rows_type, panel_type, outbox],
+        [nbr_type, panel_owner.shape], 6 + band_size,
+        neighbour_ids, panel_owner, filter_block, sends, rotation_rows,
+    )
+    coefficients = lax.psum_scatter(panels, "band", scatter_dimension=0, tiled=True)[0]
     incoming = swap(outgoing, "mesh")
-    copies_type = ((band_size,) + rotation_rows.shape, half)
-
     def gather(field):
         return call(
-            gather_kernel, "gather", [columns + (hbm,), copies_type + (hbm,)],
-            [field_type, map_type, rows_type, columns, table], [], 4 + band_size,
-            field, cell_map, rotation_rows,
+            gather_kernel, "gather", [columns + (hbm,)],
+            [field_type, map_type, columns, table], [], 3, field, cell_map,
         )
 
-    own, row_copies = gather(filter_block)
+    (own,) = gather(filter_block)
     field_one, outgoing = call(
         first_kernel, "first", [field_type + (hbm,), outbox + (hbm,)],
         inner + [field_type, pot_type, send_type, field_type, table, total, outbox],
         [nbr_type], 11, neighbour_ids, own, incoming, cell_map, cell_kernel, scale,
         filter_block, pot, sends, free=2,
     )
-    all_rows = swap(row_copies, "band")
-    outgoing, all_rows = lax.optimization_barrier((outgoing, all_rows))
     incoming = swap(outgoing, "mesh")
-    own, _ = gather(field_one)
+    (own,) = gather(field_one)
     products, energy = call(
         energy_kernel, "energy", [columns + (hbm,), ((mesh_size, 1, 128), full, vmem)],
         inner + [field_type, pot_type, columns], [nbr_type], 9,
@@ -500,11 +512,11 @@
     (rotated,) = call(
         rotate_kernel, "rotate", [rotated_type + (hbm,)],
         [
-            ((panel_owner.size * count, rotation_rows.shape[1]), half),
+            panel_type,
             ((panel_owner.size * count, width), half),
             rotated_type,
         ],
-        [panel_owner.shape], 2 + 2 * panel_owner.size, panel_owner, all_rows, states, free=2,
+        [panel_owner.shape], 3 + panel_owner.size, panel_owner, coefficients, states, free=2,
     )
     return (filtered, rotated, state_energy)
 

time: 122 us -> 124 us (1.016)
  between operations: 0.9 us -> 14.1 us
  starting transfers between devices: 49.4 us -> 41.3 us
  Pallas kernels: 57.7 us -> 54.6 us
    all_to_all x5 -> x4, starting transfers between devices: 49.4 us -> 41.3 us  [swap(): return lax.all_to_all(value, axis, split_axis=0, concat_axis=0, tiled=True)]
    pallas_call x7, Pallas kernels: 57.7 us -> 54.6 us  [call(): pl.pallas_call(kernel, out_shape=tuple((jax.ShapeDtypeStruct(dims, kind)...]
    all_to_all x5 -> x4, waiting for transfers between devices: 12.7 us -> 12.8 us  [swap(): return lax.all_to_all(value, axis, split_axis=0, concat_axis=0, tiled=True)]
  transfers between devices with their start and end apart: 5 -> 5, of which waited for: 2 -> 3; matrix products, arithmetic and copies ran while one was open for 0% -> 0% of each run, Pallas kernels for 36% -> 41%
where the time goes in v4:
time: 124 us; the launch traced here: 123 us
  Pallas kernels  54.6 us (44%)
  starting transfers between devices  41.3 us (33%)
  between operations  14.1 us (11%)
  waiting for transfers between devices  12.9 us (10%)
    pallas_call x7, Pallas kernels, call(): pl.pallas_call(kernel, out_shape=tuple((jax.ShapeDtypeStruct(dims, kind)...  54.6 us
    all_to_all x4, starting transfers between devices, swap(): return lax.all_to_all(value, axis, split_axis=0, concat_axis=0, tiled=True)  41.3 us
    all_to_all x4, waiting for transfers between devices, swap(): return lax.all_to_all(value, axis, split_axis=0, concat_axis=0, tiled=True)  12.8 us
  transfers between devices with their start and end apart: 5, of which 3 were waited for; matrix products, arithmetic and copies ran while one was open for 0% of the time, Pallas kernels for 41%

profile of v4, /device:TPU:14, one launch (start us, length us, event | category | flops | bytes accessed | tf_op | source)
XLA Modules:
  0.0 123.5 jit_solution(8813856543518651108)
XLA Ops:
  7.2 0.0 reduce-scatter.2.cloned.1.call-start
  7.2 2.6 %pack.1 = (bf16[32,16,128]{2,1,0:T(8,128)(2,1)}, bf16[16,64,512]{2,1,0:T(8,128)(2,1)}) custom-call(s32[1,14]{1,0:T(1,128)} %nbr_hbm.5, s32[2]{0:T(128)} %owner_hbm.3, bf16[32,6144]{1,0:T(8,128)(2,1)} %start_hbm.1, s32[14,1,64]{2,1,0:T(1,128)} %bitcast.8, bf16[32,512]{1,0:T(8,128)(2,1)} %rows_hbm.1), custom_call_target="tpu_custom_call" | custom-call | tf_op jit(solution)/shard_map/pack/pallas_call | solution.py:412
  9.8 0.0 reduce-scatter.2.cloned.1.call-update
  9.9 13.5 %all-to-all-start = ((bf16[32,16,128]{2,1,0:T(8,128)(2,1)}), bf16[32,16,128]{2,1,0:T(8,128)(2,1)S(1)}, u32[]{:S(2)}, u32[]{:S(2)}) async-start(bf16[32,16,128]{2,1,0:T(8,128)(2,1)} %get-tuple-element.13), calls=%async_computation | async-start | bytes 262144 | tf_op jit(solution)/shard_map/all_to_all | solution.py:429
  23.3 8.9 %gather.2.own_hbm = bf16[128,32,128]{2,1,0:T(8,128)(2,1)} custom-call(bf16[32,6144]{1,0:T(8,128)(2,1)} %start_hbm.1, s32[125,128]{1,0:T(8,128)} %map_hbm.9), custom_call_target="tpu_custom_call" | custom-call | tf_op jit(solution)/shard_map/gather/pallas_call | solution.py:412
  32.3 0.2 all-to-all-done.recv_hbm
  32.5 14.6 %first.1 = (bf16[32,6144]{1,0:T(8,128)(2,1)}, bf16[32,16,128]{2,1,0:T(8,128)(2,1)}) custom-call(s32[1,14]{1,0:T(1,128)} %nbr_hbm.5, bf16[128,32,128]{2,1,0:T(8,128)(2,1)} %gather.2.own_hbm, bf16[32,16,128]{2,1,0:T(8,128)(2,1)S(1)} %all-to-all-done.recv_hbm, s32[125,128]{1,0:T(8,128)} %map_hbm.9, bf16[125,125]{1,0:T(8,128)(2,1)} %kernel_hbm.3, ...), custom_call_target="tpu_custom_call" | custom-call | tf_op jit(solution)/shard_map/first/pallas_call | solution.py:412
  47.0 9.7 %all-to-all-start.1 = ((bf16[32,16,128]{2,1,0:T(8,128)(2,1)}), bf16[32,16,128]{2,1,0:T(8,128)(2,1)S(1)}, u32[]{:S(2)}, u32[]{:S(2)}) async-start(bf16[32,16,128]{2,1,0:T(8,128)(2,1)} %get-tuple-element.15), calls=%async_computation.1 | async-start | bytes 262144 | tf_op jit(solution)/shard_map/all_to_all | solution.py:429
  56.7 8.9 %gather.3.own_hbm = bf16[128,32,128]{2,1,0:T(8,128)(2,1)} custom-call(bf16[32,6144]{1,0:T(8,128)(2,1)} %get-tuple-element.14.field_hbm, s32[125,128]{1,0:T(8,128)} %map_hbm.9), custom_call_target="tpu_custom_call" | custom-call | tf_op jit(solution)/shard_map/gather/pallas_call | solution.py:412
  65.6 0.2 all-to-all-done.1.recv_hbm
  65.9 8.2 %energy.1 = (bf16[128,32,128]{2,1,0:T(8,128)(2,1)}, f32[32,1,128]{2,1,0:T(1,128)}) custom-call(s32[1,14]{1,0:T(1,128)} %nbr_hbm.5, bf16[128,32,128]{2,1,0:T(8,128)(2,1)} %gather.3.own_hbm, bf16[32,16,128]{2,1,0:T(8,128)(2,1)S(1)} %all-to-all-done.1.recv_hbm, s32[125,128]{1,0:T(8,128)} %map_hbm.9, bf16[125,125]{1,0:T(8,128)(2,1)} %kernel_hbm.3, ...), custom_call_target="tpu_custom_call" | custom-call | tf_op jit(solution)/shard_map/energy/pallas_call | solution.py:412
  74.1 9.6 %all-to-all-start.2 = ((f32[32,1,128]{2,1,0:T(1,128)}), f32[32,1,128]{2,1,0:T(1,128)S(1)}, u32[]{:S(2)}, u32[]{:S(2)}) async-start(f32[32,1,128]{2,1,0:T(1,128)} %get-tuple-element.20), calls=%async_computation.3 | async-start | bytes 32768 | tf_op jit(solution)/shard_map/all_to_all | solution.py:429
  83.7 9.5 %second.1 = (bf16[32,6144]{1,0:T(8,128)(2,1)}, bf16[16,32,384]{2,1,0:T(8,128)(2,1)}) custom-call(bf16[32,6144]{1,0:T(8,128)(2,1)} %get-tuple-element.14.field_hbm, bf16[128,32,128]{2,1,0:T(8,128)(2,1)} %get-tuple-element.16.cells_hbm, s32[125,128]{1,0:T(8,128)} %map_hbm.9, f32[1,6144]{1,0:T(1,128)} %bitcast.6, bf16[32,6144]{1,0:T(8,128)(2,1)} %start_hbm.1), custom_call_target="tpu_custom_call" | custom-call | tf_op jit(solution)/shard_map/second/pallas_call | solution.py:412
  93.2 0.0 all-to-all-done.2
  93.2 8.5 %all-to-all-start.3 = ((bf16[16,32,384]{2,1,0:T(8,128)(2,1)}), bf16[16,32,384]{2,1,0:T(8,128)(2,1)S(1)}, u32[]{:S(2)}, u32[]{:S(2)}) async-start(bf16[16,32,384]{2,1,0:T(8,128)(2,1)} %get-tuple-element.21), calls=%async_computation.4 | async-start | bytes 786432 | tf_op jit(solution)/shard_map/all_to_all | solution.py:429
  101.7 0.1 slice_reduce_fusion
  101.8 0.5 broadcast_multiply_fusion
  102.3 12.4 %all-to-all-done.3.states_hbm = bf16[16,32,384]{2,1,0:T(8,128)(2,1)S(1)} async-done(((bf16[16,32,384]{2,1,0:T(8,128)(2,1)}), bf16[16,32,384]{2,1,0:T(8,128)(2,1)S(1)}, u32[]{:S(2)}, u32[]{:S(2)}) %all-to-all-start.3) | async-done | bytes 393248 | tf_op jit(solution)/shard_map/all_to_all | solution.py:429
  114.7 0.0 reduce-scatter.2.cloned.1.call-done
  114.7 1.9 %rotate.1 = bf16[512,384]{1,0:T(8,128)(2,1)} custom-call(s32[2]{0:T(128)} %owner_hbm.3, bf16[64,512]{1,0:T(8,128)(2,1)} %bitcast.7, bf16[16,32,384]{2,1,0:T(8,128)(2,1)S(1)} %all-to-all-done.3.states_hbm), custom_call_target="tpu_custom_call" | custom-call | tf_op jit(solution)/shard_map/rotate/pallas_call | solution.py:412
Async XLA Ops:
  7.2 107.6 %reduce-scatter.2.cloned.1.call-start = ((), (), s32[]{:S(2)}) async-start(), calls=%async_computation.5 | async-start | bytes 1114112 | tf_op jit(solution)/shard_map/reduce_scatter | solution.py:479
  9.9 22.6 %all-to-all-start = ((bf16[32,16,128]{2,1,0:T(8,128)(2,1)}), bf16[32,16,128]{2,1,0:T(8,128)(2,1)S(1)}, u32[]{:S(2)}, u32[]{:S(2)}) async-start(bf16[32,16,128]{2,1,0:T(8,128)(2,1)} %get-tuple-element.13), calls=%async_computation | async-start | bytes 262144 | tf_op jit(solution)/shard_map/all_to_all | solution.py:429
  47.0 18.8 %all-to-all-start.1 = ((bf16[32,16,128]{2,1,0:T(8,128)(2,1)}), bf16[32,16,128]{2,1,0:T(8,128)(2,1)S(1)}, u32[]{:S(2)}, u32[]{:S(2)}) async-start(bf16[32,16,128]{2,1,0:T(8,128)(2,1)} %get-tuple-element.15), calls=%async_computation.1 | async-start | bytes 262144 | tf_op jit(solution)/shard_map/all_to_all | solution.py:429
  74.1 19.2 %all-to-all-start.2 = ((f32[32,1,128]{2,1,0:T(1,128)}), f32[32,1,128]{2,1,0:T(1,128)S(1)}, u32[]{:S(2)}, u32[]{:S(2)}) async-start(f32[32,1,128]{2,1,0:T(1,128)} %get-tuple-element.20), calls=%async_computation.3 | async-start | bytes 32768 | tf_op jit(solution)/shard_map/all_to_all | solution.py:429
  93.2 21.5 %all-to-all-start.3 = ((bf16[16,32,384]{2,1,0:T(8,128)(2,1)}), bf16[16,32,384]{2,1,0:T(8,128)(2,1)S(1)}, u32[]{:S(2)}, u32[]{:S(2)}) async-start(bf16[16,32,384]{2,1,0:T(8,128)(2,1)} %get-tuple-element.21), calls=%async_computation.4 | async-start | bytes 786432 | tf_op jit(solution)/shard_map/all_to_all | solution.py:429
Sparse Core Ops, SparseCore 0:
  10.8 75.5 reduce-scatter.1

commit v5 on v3

--- a/solution.py
+++ b/solution.py
@@ -10,16 +10,17 @@
 LO = 512
 GLO = 128
 STEP = 8
-UNROLL = 4
-
-
-def sweep(steps, body):
+UNROLL = 16
+SHORT = 8
+
+
+def sweep(steps, body, unroll):
     def group(number, carry):
-        for place in range(UNROLL):
-            body(number * UNROLL + place)
+        for place in range(unroll):
+            body(number * unroll + place)
         return carry
 
-    lax.fori_loop(0, steps // UNROLL, group, 0)
+    lax.fori_loop(0, steps // unroll, group, 0)
 
 
 def flags(row, width):
@@ -154,7 +155,7 @@
         block = block_of(map_ref, number)
         gather_chunk(table_ref[...], block, marks_of(block, LO), own_ref, number, count)
 
-    sweep(map_ref.shape[0] // STEP, body)
+    sweep(map_ref.shape[0] // STEP, body, SHORT)
     copies.start(own_ref, own_hbm).wait()
     for copy in pending:
         copy.wait()
@@ -207,7 +208,7 @@
             base = number * STEP + k
             nodes_ref[base] = part + own_ref[base].astype(jnp.float32)
 
-    sweep(map_ref.shape[0] // STEP, body)
+    sweep(map_ref.shape[0] // STEP, body, UNROLL)
     kernel_copy.wait()
     square_ref[:npe, :npe] = kernel_ref[...]
     scale_copy.wait()
@@ -248,7 +249,7 @@
             preferred_element_type=jnp.float32,
         )
 
-    sweep(map_ref.shape[0] // STEP, body)
+    sweep(map_ref.shape[0] // STEP, body, UNROLL)
 
 
 def first_kernel(
@@ -328,7 +329,7 @@
 
 
 def second_kernel(
-    field_hbm, cells_hbm, map_hbm, pot_hbm, start_hbm, next_hbm, out_hbm,
+    field_hbm, cells_hbm, map_hbm, pot_hbm, start_hbm, next_hbm, out_ref,
     field_ref, cells_ref, map_ref, pot_ref, start_ref, next_ref, total_ref, sems,
 ):
     copies = Copies(sems)
@@ -355,19 +356,17 @@
         next_ref[:, lanes] = (
             2.0 * (image - center * one) / half_width - start
         ).astype(jnp.bfloat16)
-    width = out_hbm.shape[2]
-    pending = [copies.start(next_ref, next_hbm)]
-    for band in range(out_hbm.shape[0]):
-        pending.append(
-            copies.start(next_ref.at[:, band * width : (band + 1) * width], out_hbm.at[band])
-        )
-    for copy in pending:
-        copy.wait()
-
-
-def rotate_kernel(owner_hbm, rows_hbm, states_hbm, out_hbm, rows_ref, states_ref, out_ref, owner_ref, sems):
+    next_copy = copies.start(next_ref, next_hbm)
+    width = out_ref.shape[2]
+    for band in range(out_ref.shape[0]):
+        out_ref[band] = next_ref[:, band * width : (band + 1) * width]
+    next_copy.wait()
+
+
+def rotate_kernel(
+    owner_ref, rows_hbm, states_hbm, out_hbm, rows_ref, states_ref, out_ref, sems
+):
     copies = Copies(sems)
-    copies.start(owner_hbm, owner_ref).wait()
     pending = []
     count = rows_hbm.shape[1]
     for k in range(owner_ref.shape[0]):
@@ -385,15 +384,16 @@
 
 vmem = pl.BlockSpec(memory_space=pltpu.VMEM)
 hbm = pl.BlockSpec(memory_space=pltpu.HBM)
+smem = pl.BlockSpec(memory_space=pltpu.SMEM)
 anywhere = pl.BlockSpec(memory_space=pl.ANY)
 half = jnp.bfloat16
 full = jnp.float32
 whole = jnp.int32
 
 
-def call(kernel, name, outs, scratch, scalars, sems, *operands, free=-1):
+def call(kernel, name, outs, scratch, scalars, sems, *operands, free=-1, number=-1):
     held = [
-        value if k == free else pltpu.with_memory_space_constraint(value, pltpu.HBM)
+        value if k in (free, number) else pltpu.with_memory_space_constraint(value, pltpu.HBM)
         for k, value in enumerate(operands)
     ]
     return pl.pallas_call(
@@ -402,7 +402,9 @@
             jax.ShapeDtypeStruct(dims, kind) if place is vmem else pltpu.HBM(dims, kind)
             for dims, kind, place in outs
         ),
-        in_specs=[anywhere if k == free else hbm for k in range(len(operands))],
+        in_specs=[
+            anywhere if k == free else smem if k == number else hbm for k in range(len(operands))
+        ],
         out_specs=tuple(place for _, _, place in outs),
         scratch_shapes=[pltpu.VMEM(dims, kind) for dims, kind in scratch]
         + [pltpu.SMEM(dims, jnp.int32) for dims in scalars]
@@ -489,13 +491,13 @@
     energies = swap(energy, "mesh")
     filtered, parts = call(
         second_kernel, "second",
-        [field_type + (hbm,), ((band_size, count, width), half, hbm)],
+        [field_type + (hbm,), ((band_size, count, width), half, vmem)],
         [field_type, columns, map_type, pot_type, field_type, field_type, total],
-        [], 6 + band_size, field_one, products, cell_map, pot, filter_block,
-    )
-    parts, energies = lax.optimization_barrier((parts, energies))
+        [], 6, field_one, products, cell_map, pot, filter_block,
+    )
+    state_energy = jnp.sum(energies[:, 0, :count], axis=0) / (nodes * mesh_size)
+    parts, state_energy = lax.optimization_barrier((parts, state_energy))
     states = swap(parts, "band")
-    state_energy = jnp.sum(energies[:, 0, :count], axis=0) / (nodes * mesh_size)
     rotated_type = ((rotation_rows.shape[1], width), half)
     (rotated,) = call(
         rotate_kernel, "rotate", [rotated_type + (hbm,)],
@@ -504,7 +506,7 @@
             ((panel_owner.size * count, width), half),
             rotated_type,
         ],
-        [panel_owner.shape], 2 + 2 * panel_owner.size, panel_owner, all_rows, states, free=2,
+        [], 1 + 2 * panel_owner.size, panel_owner, all_rows, states, free=2, number=0,
     )
     return (filtered, rotated, state_energy)
 

time: 122 us -> 119 us (0.975)
  blocking collectives: 0 us -> 19.7 us
  waiting for transfers between devices: 12.7 us -> 1.37 us
  starting transfers between devices: 49.4 us -> 41.6 us
  Pallas kernels: 57.7 us -> 54.4 us
    all_to_all x0 -> x1, blocking collectives: none -> 19.7 us  [swap(): return lax.all_to_all(value, axis, split_axis=0, concat_axis=0, tiled=True)]
    all_to_all x5 -> x4, waiting for transfers between devices: 12.7 us -> 1.37 us  [swap(): return lax.all_to_all(value, axis, split_axis=0, concat_axis=0, tiled=True)]
    all_to_all x5 -> x4, starting transfers between devices: 49.4 us -> 41.6 us  [swap(): return lax.all_to_all(value, axis, split_axis=0, concat_axis=0, tiled=True)]
    pallas_call x7, Pallas kernels: 57.7 us -> 54.4 us  [call(): pl.pallas_call(kernel, out_shape=tuple((jax.ShapeDtypeStruct(dims, kind)...]
  transfers between devices with their start and end apart: 5 -> 4, of which waited for: 2 -> 1; matrix products, arithmetic and copies ran while one was open for 0% -> 0% of each run, Pallas kernels for 36% -> 35%
where the time goes in v5:
time: 119 us
  Pallas kernels  54.4 us (46%)
  starting transfers between devices  41.6 us (35%)
  blocking collectives  19.7 us (17%)
  waiting for transfers between devices  1.37 us (1%)
    pallas_call x7, Pallas kernels, call(): pl.pallas_call(kernel, out_shape=tuple((jax.ShapeDtypeStruct(dims, kind)...  54.4 us
    all_to_all x4, starting transfers between devices, swap(): return lax.all_to_all(value, axis, split_axis=0, concat_axis=0, tiled=True)  41.6 us
    all_to_all x1, blocking collectives, swap(): return lax.all_to_all(value, axis, split_axis=0, concat_axis=0, tiled=True)  19.7 us
  transfers between devices with their start and end apart: 4, of which 1 were waited for; matrix products, arithmetic and copies ran while one was open for 0% of the time, Pallas kernels for 35%

profile of v5, /device:TPU:14, one launch (start us, length us, event | category | flops | bytes accessed | tf_op | source)
XLA Modules:
  0.0 118.6 jit_solution(8478277782299854745)
XLA Ops:
  0.6 2.5 %pack.1 = bf16[32,16,128]{2,1,0:T(8,128)(2,1)} custom-call(s32[1,14]{1,0:T(1,128)} %nbr_hbm.5, bf16[32,6144]{1,0:T(8,128)(2,1)} %start_hbm.1, s32[14,1,64]{2,1,0:T(1,128)} %bitcast.6), custom_call_target="tpu_custom_call" | custom-call | tf_op jit(solution)/shard_map/pack/pallas_call | solution.py:399
  3.1 13.5 %all-to-all-start = ((bf16[32,16,128]{2,1,0:T(8,128)(2,1)}), bf16[32,16,128]{2,1,0:T(8,128)(2,1)S(1)}, u32[]{:S(2)}, u32[]{:S(2)}) async-start(bf16[32,16,128]{2,1,0:T(8,128)(2,1)} %pack.1), calls=%async_computation | async-start | bytes 262144 | tf_op jit(solution)/shard_map/all_to_all | solution.py:418
  16.6 9.1 %gather.2 = (bf16[128,32,128]{2,1,0:T(8,128)(2,1)}, bf16[16,32,512]{2,1,0:T(8,128)(2,1)}) custom-call(bf16[32,6144]{1,0:T(8,128)(2,1)} %start_hbm.1, s32[125,128]{1,0:T(8,128)} %map_hbm.9, bf16[32,512]{1,0:T(8,128)(2,1)} %rows_hbm.3), custom_call_target="tpu_custom_call" | custom-call | tf_op jit(solution)/shard_map/gather/pallas_call | solution.py:399
  25.7 0.0 all-to-all-done.recv_hbm
  25.7 8.5 %all-to-all-start.1 = ((bf16[16,32,512]{2,1,0:T(8,128)(2,1)}), bf16[16,32,512]{2,1,0:T(8,128)(2,1)S(1)}, u32[]{:S(2)}, u32[]{:S(2)}) async-start(bf16[16,32,512]{2,1,0:T(8,128)(2,1)} %get-tuple-element.20), calls=%async_computation.1 | async-start | bytes 1048576 | tf_op jit(solution)/shard_map/all_to_all | solution.py:418
  34.2 14.3 %first.1 = (bf16[32,6144]{1,0:T(8,128)(2,1)}, bf16[32,16,128]{2,1,0:T(8,128)(2,1)}) custom-call(s32[1,14]{1,0:T(1,128)} %nbr_hbm.5, bf16[128,32,128]{2,1,0:T(8,128)(2,1)} %get-tuple-element.16.own_hbm, bf16[32,16,128]{2,1,0:T(8,128)(2,1)S(1)} %all-to-all-done.recv_hbm, s32[125,128]{1,0:T(8,128)} %map_hbm.9, bf16[125,125]{1,0:T(8,128)(2,1)} %kernel_hbm.3, ...), custom_call_target="tpu_custom_call" | custom-call | tf_op jit(solution)/shard_map/first/pallas_call | solution.py:399
  48.5 1.3 %all-to-all-done.1.rows_hbm = bf16[16,32,512]{2,1,0:T(8,128)(2,1)S(1)} async-done(((bf16[16,32,512]{2,1,0:T(8,128)(2,1)}), bf16[16,32,512]{2,1,0:T(8,128)(2,1)S(1)}, u32[]{:S(2)}, u32[]{:S(2)}) %all-to-all-start.1) | async-done | bytes 524320 | tf_op jit(solution)/shard_map/all_to_all | solution.py:418
  49.8 0.0 copy-start.1
  49.8 9.8 %all-to-all-start.2 = ((bf16[32,16,128]{2,1,0:T(8,128)(2,1)}), bf16[32,16,128]{2,1,0:T(8,128)(2,1)S(1)}, u32[]{:S(2)}, u32[]{:S(2)}) async-start(bf16[32,16,128]{2,1,0:T(8,128)(2,1)} %get-tuple-element.21), calls=%async_computation.2 | async-start | bytes 262144 | tf_op jit(solution)/shard_map/all_to_all | solution.py:418
  59.6 9.1 %gather.3 = (bf16[128,32,128]{2,1,0:T(8,128)(2,1)}, bf16[16,32,512]{2,1,0:T(8,128)(2,1)}) custom-call(bf16[32,6144]{1,0:T(8,128)(2,1)} %get-tuple-element.17.field_hbm, s32[125,128]{1,0:T(8,128)} %map_hbm.9, bf16[32,512]{1,0:T(8,128)(2,1)} %rows_hbm.3), custom_call_target="tpu_custom_call" | custom-call | tf_op jit(solution)/shard_map/gather/pallas_call | solution.py:399
  68.7 0.0 all-to-all-done.2.recv_hbm
  68.7 8.0 %energy.1 = (bf16[128,32,128]{2,1,0:T(8,128)(2,1)}, f32[32,1,128]{2,1,0:T(1,128)}) custom-call(s32[1,14]{1,0:T(1,128)} %nbr_hbm.5, bf16[128,32,128]{2,1,0:T(8,128)(2,1)} %get-tuple-element.18.own_hbm, bf16[32,16,128]{2,1,0:T(8,128)(2,1)S(1)} %all-to-all-done.2.recv_hbm, s32[125,128]{1,0:T(8,128)} %map_hbm.9, bf16[125,125]{1,0:T(8,128)(2,1)} %kernel_hbm.3, ...), custom_call_target="tpu_custom_call" | custom-call | tf_op jit(solution)/shard_map/energy/pallas_call | solution.py:399
  76.8 0.0 copy-done.1
  76.8 9.8 %all-to-all-start.3 = ((f32[32,1,128]{2,1,0:T(1,128)}), f32[32,1,128]{2,1,0:T(1,128)S(1)}, u32[]{:S(2)}, u32[]{:S(2)}) async-start(f32[32,1,128]{2,1,0:T(1,128)} %get-tuple-element.26), calls=%async_computation.3 | async-start | bytes 32768 | tf_op jit(solution)/shard_map/all_to_all | solution.py:418
  86.6 9.0 %second.1 = (bf16[32,6144]{1,0:T(8,128)(2,1)}, bf16[16,32,384]{2,1,0:T(8,128)(2,1)S(1)}) custom-call(bf16[32,6144]{1,0:T(8,128)(2,1)} %get-tuple-element.17.field_hbm, bf16[128,32,128]{2,1,0:T(8,128)(2,1)} %get-tuple-element.22.cells_hbm, s32[125,128]{1,0:T(8,128)} %map_hbm.9, f32[1,6144]{1,0:T(1,128)} %bitcast.5, bf16[32,6144]{1,0:T(8,128)(2,1)} %start_hbm.1), custom_call_target="tpu_custom_call" | custom-call | tf_op jit(solution)/shard_map/second/pallas_call | solution.py:399
  95.6 0.0 all-to-all-done.3
  95.6 0.1 slice_reduce_fusion
  95.7 0.5 broadcast_multiply_fusion
  96.2 0.0 copy-start
  96.2 19.7 %all_to_all.25.states_hbm = bf16[16,32,384]{2,1,0:T(8,128)(2,1)S(1)} all-to-all(bf16[16,32,384]{2,1,0:T(8,128)(2,1)S(1)} %get-tuple-element.27), channel_id=1, replica_groups=mesh['mesh'=32,'band'=16] {'band'}, dimensions={0} | all-to-all | bytes 786432 | tf_op jit(solution)/shard_map/all_to_all | solution.py:418
  116.0 0.0 copy-done
  116.0 2.4 %rotate.1 = bf16[512,384]{1,0:T(8,128)(2,1)} custom-call(s32[2]{0:T(128)S(1)} %copy-done, bf16[16,32,512]{2,1,0:T(8,128)(2,1)} %copy-done.1, bf16[16,32,384]{2,1,0:T(8,128)(2,1)S(1)} %all_to_all.25.states_hbm), custom_call_target="tpu_custom_call" | custom-call | tf_op jit(solution)/shard_map/rotate/pallas_call | solution.py:399
Async XLA Ops:
  3.1 22.6 %all-to-all-start = ((bf16[32,16,128]{2,1,0:T(8,128)(2,1)}), bf16[32,16,128]{2,1,0:T(8,128)(2,1)S(1)}, u32[]{:S(2)}, u32[]{:S(2)}) async-start(bf16[32,16,128]{2,1,0:T(8,128)(2,1)} %pack.1), calls=%async_computation | async-start | bytes 262144 | tf_op jit(solution)/shard_map/all_to_all | solution.py:418
  25.7 24.1 %all-to-all-start.1 = ((bf16[16,32,512]{2,1,0:T(8,128)(2,1)}), bf16[16,32,512]{2,1,0:T(8,128)(2,1)S(1)}, u32[]{:S(2)}, u32[]{:S(2)}) async-start(bf16[16,32,512]{2,1,0:T(8,128)(2,1)} %get-tuple-element.20), calls=%async_computation.1 | async-start | bytes 1048576 | tf_op jit(solution)/shard_map/all_to_all | solution.py:418
  49.8 27.0 %copy-start.1 = (bf16[16,32,512]{2,1,0:T(8,128)(2,1)}, bf16[16,32,512]{2,1,0:T(8,128)(2,1)S(1)}, u32[]{:S(2)}) copy-start(bf16[16,32,512]{2,1,0:T(8,128)(2,1)S(1)} %all-to-all-done.1.rows_hbm) | copy-start | bytes 1572868
  49.8 19.0 %all-to-all-start.2 = ((bf16[32,16,128]{2,1,0:T(8,128)(2,1)}), bf16[32,16,128]{2,1,0:T(8,128)(2,1)S(1)}, u32[]{:S(2)}, u32[]{:S(2)}) async-start(bf16[32,16,128]{2,1,0:T(8,128)(2,1)} %get-tuple-element.21), calls=%async_computation.2 | async-start | bytes 262144 | tf_op jit(solution)/shard_map/all_to_all | solution.py:418
  76.8 18.9 %all-to-all-start.3 = ((f32[32,1,128]{2,1,0:T(1,128)}), f32[32,1,128]{2,1,0:T(1,128)S(1)}, u32[]{:S(2)}, u32[]{:S(2)}) async-start(f32[32,1,128]{2,1,0:T(1,128)} %get-tuple-element.26), calls=%async_computation.3 | async-start | bytes 32768 | tf_op jit(solution)/shard_map/all_to_all | solution.py:418
  96.2 19.7 %copy-start = (s32[2]{0:T(128)S(1)}, s32[2]{0:T(128)}, u32[]{:S(2)}) copy-start(s32[2]{0:T(128)} %owner_ref.1) | copy-start | bytes 28

commit v6 on v5

--- a/solution.py
+++ b/solution.py
@@ -12,6 +12,7 @@
 STEP = 8
 UNROLL = 16
 SHORT = 8
+PIECE = 32
 
 
 def sweep(steps, body, unroll):
@@ -20,7 +21,10 @@
             body(number * unroll + place)
         return carry
 
-    lax.fori_loop(0, steps // unroll, group, 0)
+    if steps == unroll:
+        group(0, 0)
+    else:
+        lax.fori_loop(0, steps // unroll, group, 0)
 
 
 def flags(row, width):
@@ -95,7 +99,10 @@
 
 
 def block_of(ref, number):
-    return ref[pl.ds(pl.multiple_of(number * STEP, STEP), STEP), :]
+    base = number * STEP
+    if not isinstance(base, int):
+        base = pl.multiple_of(base, STEP)
+    return ref[pl.ds(base, STEP), :]
 
 
 def pack_sends(table_ref, send_ref, nbr_ref, out_ref, count):
@@ -310,11 +317,14 @@
         ghost_ref, square_ref, nodes_ref, product_ref, nbr_ref, nodes, later,
     )
     total = jnp.zeros((count, 128), jnp.float32)
+    pending = []
     for base in range(own_ref.shape[0]):
         value = product_ref[base]
         cells_ref[base] = value.astype(jnp.bfloat16)
         total = total + value * own_ref[base].astype(jnp.float32)
-    cells_copy = copies.start(cells_ref, cells_hbm)
+        if (base + 1) % PIECE == 0:
+            piece = slice(base + 1 - PIECE, base + 1)
+            pending.append(copies.start(cells_ref.at[piece], cells_hbm.at[piece]))
     for copy in others:
         copy.wait()
     for base in range(0, nodes, 128):
@@ -325,7 +335,8 @@
     lane = lax.broadcasted_iota(jnp.int32, total.shape, 1)
     line = jnp.sum(jnp.where(state == lane, sums, 0.0), axis=0, keepdims=True)
     energy_ref[...] = jnp.broadcast_to(line[None], energy_ref.shape)
-    cells_copy.wait()
+    for copy in pending:
+        copy.wait()
 
 
 def second_kernel(
@@ -363,23 +374,21 @@
     next_copy.wait()
 
 
-def rotate_kernel(
-    owner_ref, rows_hbm, states_hbm, out_hbm, rows_ref, states_ref, out_ref, sems
-):
+def rotate_kernel(owner_ref, rows_ref, states_ref, out_hbm, out_ref, sems):
     copies = Copies(sems)
+    owners = [owner_ref[k] for k in range(owner_ref.shape[0])]
+    rows = jnp.concatenate([rows_ref[owner] for owner in owners], axis=0)
+    panels = jnp.concatenate([states_ref[owner] for owner in owners], axis=0)
+    size = out_ref.shape[0] // 2
     pending = []
-    count = rows_hbm.shape[1]
-    for k in range(owner_ref.shape[0]):
-        place = pl.ds(k * count, count)
-        pending.append(copies.start(rows_hbm.at[owner_ref[k]], rows_ref.at[place]))
-        pending.append(copies.start(states_hbm.at[owner_ref[k]], states_ref.at[place]))
+    for side in range(2):
+        piece = slice(side * size, (side + 1) * size)
+        out_ref[piece, :] = lax.dot_general(
+            rows[:, piece], panels, (((0,), (0,)), ((), ())), preferred_element_type=jnp.float32
+        ).astype(jnp.bfloat16)
+        pending.append(copies.start(out_ref.at[piece], out_hbm.at[piece]))
     for copy in pending:
         copy.wait()
-    out_ref[...] = lax.dot_general(
-        rows_ref[...], states_ref[...], (((0,), (0,)), ((), ())),
-        preferred_element_type=jnp.float32,
-    ).astype(jnp.bfloat16)
-    copies.start(out_ref, out_hbm).wait()
 
 
 vmem = pl.BlockSpec(memory_space=pltpu.VMEM)
@@ -391,10 +400,12 @@
 whole = jnp.int32
 
 
-def call(kernel, name, outs, scratch, scalars, sems, *operands, free=-1, number=-1):
+def call(kernel, name, outs, scratch, scalars, sems, *operands, free=-1, places=None):
+    if places is None:
+        places = [anywhere if k == free else hbm for k in range(len(operands))]
     held = [
-        value if k in (free, number) else pltpu.with_memory_space_constraint(value, pltpu.HBM)
-        for k, value in enumerate(operands)
+        pltpu.with_memory_space_constraint(value, pltpu.HBM) if place is hbm else value
+        for place, value in zip(places, operands)
     ]
     return pl.pallas_call(
         kernel,
@@ -402,9 +413,7 @@
             jax.ShapeDtypeStruct(dims, kind) if place is vmem else pltpu.HBM(dims, kind)
             for dims, kind, place in outs
         ),
-        in_specs=[
-            anywhere if k == free else smem if k == number else hbm for k in range(len(operands))
-        ],
+        in_specs=list(places),
         out_specs=tuple(place for _, _, place in outs),
         scratch_shapes=[pltpu.VMEM(dims, kind) for dims, kind in scratch]
         + [pltpu.SMEM(dims, jnp.int32) for dims in scalars]
@@ -485,7 +494,7 @@
     own, _ = gather(field_one)
     products, energy = call(
         energy_kernel, "energy", [columns + (hbm,), ((mesh_size, 1, 128), full, vmem)],
-        inner + [field_type, pot_type, columns], [nbr_type], 9,
+        inner + [field_type, pot_type, columns], [nbr_type], 8 + padded // PIECE,
         neighbour_ids, own, incoming, cell_map, cell_kernel, scale, field_one, pot, free=2,
     )
     energies = swap(energy, "mesh")
@@ -500,13 +509,8 @@
     states = swap(parts, "band")
     rotated_type = ((rotation_rows.shape[1], width), half)
     (rotated,) = call(
-        rotate_kernel, "rotate", [rotated_type + (hbm,)],
-        [
-            ((panel_owner.size * count, rotation_rows.shape[1]), half),
-            ((panel_owner.size * count, width), half),
-            rotated_type,
-        ],
-        [], 1 + 2 * panel_owner.size, panel_owner, all_rows, states, free=2, number=0,
+        rotate_kernel, "rotate", [rotated_type + (hbm,)], [rotated_type], [], 2,
+        panel_owner, all_rows, states, places=(smem, vmem, vmem),
     )
     return (filtered, rotated, state_energy)
 

time: 119 us -> 118 us (level)
  no operation moved by 1% of the time
where the time goes in v6:
time: 118 us; the launch traced here: 117 us
  Pallas kernels  53.4 us (45%)
  starting transfers between devices  41.6 us (35%)
  blocking collectives  19.7 us (17%)
  waiting for transfers between devices  1.37 us (1%)
    pallas_call x7, Pallas kernels, call(): pl.pallas_call(kernel, out_shape=tuple((jax.ShapeDtypeStruct(dims, kind)...  53.4 us
    all_to_all x4, starting transfers between devices, swap(): return lax.all_to_all(value, axis, split_axis=0, concat_axis=0, tiled=True)  41.6 us
    all_to_all x1, blocking collectives, swap(): return lax.all_to_all(value, axis, split_axis=0, concat_axis=0, tiled=True)  19.7 us
  transfers between devices with their start and end apart: 4, of which 1 were waited for; matrix products, arithmetic and copies ran while one was open for 0% of the time, Pallas kernels for 35%

profile of v6, /device:TPU:14, one launch (start us, length us, event | category | flops | bytes accessed | tf_op | source)
XLA Modules:
  0.0 117.5 jit_solution(7384988750141383223)
XLA Ops:
  0.6 2.5 %pack.1 = bf16[32,16,128]{2,1,0:T(8,128)(2,1)} custom-call(s32[1,14]{1,0:T(1,128)} %nbr_hbm.5, bf16[32,6144]{1,0:T(8,128)(2,1)} %start_hbm.1, s32[14,1,64]{2,1,0:T(1,128)} %bitcast.6), custom_call_target="tpu_custom_call" | custom-call | tf_op jit(solution)/shard_map/pack/pallas_call | solution.py:410
  3.1 13.5 %all-to-all-start = ((bf16[32,16,128]{2,1,0:T(8,128)(2,1)}), bf16[32,16,128]{2,1,0:T(8,128)(2,1)S(1)}, u32[]{:S(2)}, u32[]{:S(2)}) async-start(bf16[32,16,128]{2,1,0:T(8,128)(2,1)} %pack.1), calls=%async_computation | async-start | bytes 262144 | tf_op jit(solution)/shard_map/all_to_all | solution.py:427
  16.6 9.1 %gather.2 = (bf16[128,32,128]{2,1,0:T(8,128)(2,1)}, bf16[16,32,512]{2,1,0:T(8,128)(2,1)}) custom-call(bf16[32,6144]{1,0:T(8,128)(2,1)} %start_hbm.1, s32[125,128]{1,0:T(8,128)} %map_hbm.9, bf16[32,512]{1,0:T(8,128)(2,1)} %rows_hbm.3), custom_call_target="tpu_custom_call" | custom-call | tf_op jit(solution)/shard_map/gather/pallas_call | solution.py:410
  25.7 0.0 all-to-all-done.recv_hbm
  25.7 8.5 %all-to-all-start.1 = ((bf16[16,32,512]{2,1,0:T(8,128)(2,1)}), bf16[16,32,512]{2,1,0:T(8,128)(2,1)S(1)}, u32[]{:S(2)}, u32[]{:S(2)}) async-start(bf16[16,32,512]{2,1,0:T(8,128)(2,1)} %get-tuple-element.20), calls=%async_computation.1 | async-start | bytes 1048576 | tf_op jit(solution)/shard_map/all_to_all | solution.py:427
  34.2 14.3 %first.1 = (bf16[32,6144]{1,0:T(8,128)(2,1)}, bf16[32,16,128]{2,1,0:T(8,128)(2,1)}) custom-call(s32[1,14]{1,0:T(1,128)} %nbr_hbm.5, bf16[128,32,128]{2,1,0:T(8,128)(2,1)} %get-tuple-element.16.own_hbm, bf16[32,16,128]{2,1,0:T(8,128)(2,1)S(1)} %all-to-all-done.recv_hbm, s32[125,128]{1,0:T(8,128)} %map_hbm.9, bf16[125,125]{1,0:T(8,128)(2,1)} %kernel_hbm.3, ...), custom_call_target="tpu_custom_call" | custom-call | tf_op jit(solution)/shard_map/first/pallas_call | solution.py:410
  48.5 1.3 %all-to-all-done.1.rows_ref = bf16[16,32,512]{2,1,0:T(8,128)(2,1)S(1)} async-done(((bf16[16,32,512]{2,1,0:T(8,128)(2,1)}), bf16[16,32,512]{2,1,0:T(8,128)(2,1)S(1)}, u32[]{:S(2)}, u32[]{:S(2)}) %all-to-all-start.1) | async-done | bytes 524320 | tf_op jit(solution)/shard_map/all_to_all | solution.py:427
  49.8 9.8 %all-to-all-start.2 = ((bf16[32,16,128]{2,1,0:T(8,128)(2,1)}), bf16[32,16,128]{2,1,0:T(8,128)(2,1)S(1)}, u32[]{:S(2)}, u32[]{:S(2)}) async-start(bf16[32,16,128]{2,1,0:T(8,128)(2,1)} %get-tuple-element.21), calls=%async_computation.2 | async-start | bytes 262144 | tf_op jit(solution)/shard_map/all_to_all | solution.py:427
  59.6 9.1 %gather.3 = (bf16[128,32,128]{2,1,0:T(8,128)(2,1)}, bf16[16,32,512]{2,1,0:T(8,128)(2,1)}) custom-call(bf16[32,6144]{1,0:T(8,128)(2,1)} %get-tuple-element.17.field_hbm, s32[125,128]{1,0:T(8,128)} %map_hbm.9, bf16[32,512]{1,0:T(8,128)(2,1)} %rows_hbm.3), custom_call_target="tpu_custom_call" | custom-call | tf_op jit(solution)/shard_map/gather/pallas_call | solution.py:410
  68.7 0.0 all-to-all-done.2.recv_hbm
  68.7 7.8 %energy.1 = (bf16[128,32,128]{2,1,0:T(8,128)(2,1)}, f32[32,1,128]{2,1,0:T(1,128)}) custom-call(s32[1,14]{1,0:T(1,128)} %nbr_hbm.5, bf16[128,32,128]{2,1,0:T(8,128)(2,1)} %get-tuple-element.18.own_hbm, bf16[32,16,128]{2,1,0:T(8,128)(2,1)S(1)} %all-to-all-done.2.recv_hbm, s32[125,128]{1,0:T(8,128)} %map_hbm.9, bf16[125,125]{1,0:T(8,128)(2,1)} %kernel_hbm.3, ...), custom_call_target="tpu_custom_call" | custom-call | tf_op jit(solution)/shard_map/energy/pallas_call | solution.py:410
  76.6 9.8 %all-to-all-start.3 = ((f32[32,1,128]{2,1,0:T(1,128)}), f32[32,1,128]{2,1,0:T(1,128)S(1)}, u32[]{:S(2)}, u32[]{:S(2)}) async-start(f32[32,1,128]{2,1,0:T(1,128)} %get-tuple-element.26), calls=%async_computation.3 | async-start | bytes 32768 | tf_op jit(solution)/shard_map/all_to_all | solution.py:427
  86.4 9.0 %second.1 = (bf16[32,6144]{1,0:T(8,128)(2,1)}, bf16[16,32,384]{2,1,0:T(8,128)(2,1)S(1)}) custom-call(bf16[32,6144]{1,0:T(8,128)(2,1)} %get-tuple-element.17.field_hbm, bf16[128,32,128]{2,1,0:T(8,128)(2,1)} %get-tuple-element.22.cells_hbm, s32[125,128]{1,0:T(8,128)} %map_hbm.9, f32[1,6144]{1,0:T(1,128)} %bitcast.5, bf16[32,6144]{1,0:T(8,128)(2,1)} %start_hbm.1), custom_call_target="tpu_custom_call" | custom-call | tf_op jit(solution)/shard_map/second/pallas_call | solution.py:410
  95.4 0.0 all-to-all-done.3
  95.5 0.1 slice_reduce_fusion
  95.5 0.5 broadcast_multiply_fusion
  96.0 0.0 copy-start
  96.0 19.7 %all_to_all.25.states_ref = bf16[16,32,384]{2,1,0:T(8,128)(2,1)S(1)} all-to-all(bf16[16,32,384]{2,1,0:T(8,128)(2,1)S(1)} %get-tuple-element.27), channel_id=1, replica_groups=mesh['mesh'=32,'band'=16] {'band'}, dimensions={0} | all-to-all | bytes 786432 | tf_op jit(solution)/shard_map/all_to_all | solution.py:427
  115.7 0.0 copy-done
  115.7 1.6 %rotate.1 = bf16[512,384]{1,0:T(8,128)(2,1)} custom-call(s32[2]{0:T(128)S(1)} %copy-done, bf16[16,32,512]{2,1,0:T(8,128)(2,1)S(1)} %all-to-all-done.1.rows_ref, bf16[16,32,384]{2,1,0:T(8,128)(2,1)S(1)} %all_to_all.25.states_ref), custom_call_target="tpu_custom_call" | custom-call | tf_op jit(solution)/shard_map/rotate/pallas_call | solution.py:410
Async XLA Ops:
  3.1 22.6 %all-to-all-start = ((bf16[32,16,128]{2,1,0:T(8,128)(2,1)}), bf16[32,16,128]{2,1,0:T(8,128)(2,1)S(1)}, u32[]{:S(2)}, u32[]{:S(2)}) async-start(bf16[32,16,128]{2,1,0:T(8,128)(2,1)} %pack.1), calls=%async_computation | async-start | bytes 262144 | tf_op jit(solution)/shard_map/all_to_all | solution.py:427
  25.7 24.1 %all-to-all-start.1 = ((bf16[16,32,512]{2,1,0:T(8,128)(2,1)}), bf16[16,32,512]{2,1,0:T(8,128)(2,1)S(1)}, u32[]{:S(2)}, u32[]{:S(2)}) async-start(bf16[16,32,512]{2,1,0:T(8,128)(2,1)} %get-tuple-element.20), calls=%async_computation.1 | async-start | bytes 1048576 | tf_op jit(solution)/shard_map/all_to_all | solution.py:427
  49.8 19.0 %all-to-all-start.2 = ((bf16[32,16,128]{2,1,0:T(8,128)(2,1)}), bf16[32,16,128]{2,1,0:T(8,128)(2,1)S(1)}, u32[]{:S(2)}, u32[]{:S(2)}) async-start(bf16[32,16,128]{2,1,0:T(8,128)(2,1)} %get-tuple-element.21), calls=%async_computation.2 | async-start | bytes 262144 | tf_op jit(solution)/shard_map/all_to_all | solution.py:427
  76.6 18.9 %all-to-all-start.3 = ((f32[32,1,128]{2,1,0:T(1,128)}), f32[32,1,128]{2,1,0:T(1,128)S(1)}, u32[]{:S(2)}, u32[]{:S(2)}) async-start(f32[32,1,128]{2,1,0:T(1,128)} %get-tuple-element.26), calls=%async_computation.3 | async-start | bytes 32768 | tf_op jit(solution)/shard_map/all_to_all | solution.py:427
  96.0 19.7 %copy-start = (s32[2]{0:T(128)S(1)}, s32[2]{0:T(128)}, u32[]{:S(2)}) copy-start(s32[2]{0:T(128)} %owner_ref.1) | copy-start | bytes 28
